TPU v7x, 32 devices: a whole 2x2x4 slice. The times are simulated.
32 devices in a mesh: rep: 2 (over y), head: 4 (over x, core), row: 4 (over z).
Axes of the slice: x: 2, y: 2, z: 4, core: 2. Of those that a mesh axis runs over, the one named last changes fastest.
Arguments:
- hidden: bfloat16 [256, 2, 8192], P(('rep', 'row'), None, 'head'), parts along dimension 0, may hold values from -6 to 6
- input_norm_scale: float32 [8192], P('head'), may hold values from 0.5 to 1.5
- projection_signal: bfloat16 [8192, 4096], P('row', 'head'), may hold values from -0.0625 to 0.0625
- projection_gate: bfloat16 [8192, 4096], P('row', 'head'), may hold values from -0.0625 to 0.0625
- projection_step: bfloat16 [8192, 64], P('row', 'head'), may hold values from -0.0625 to 0.0625
- projection_input_output: bfloat16 [8192, 256], P('row'), may hold values from -0.0625 to 0.0625
- step_bias: float32 [64], P('head'), may hold values from -4 to 0
- head_decay_rate: float32 [64], P('head'), may hold values from 0.5 to 16
- head_skip_weight: float32 [64], P('head'), may hold values from 0.5 to 1.5
- gated_norm_scale: float32 [4096], P('head'), may hold values from 0.5 to 1.5
- adapter_down_weight: bfloat16 [512, 8192, 16], P('row', 'head'), may hold values from -0.0625 to 0.0625
- adapter_up_weight: bfloat16 [512, 16, 4096], P('row', None, 'head'), may hold values from -1.5 to 1.5
- output_weight: bfloat16 [4096, 8192], P('head'), may hold values from -0.125 to 0.125
- scan_state: bfloat16 [256, 64, 64, 128], P(('rep', 'row'), 'head'), parts along dimension 0, may hold values from -6 to 6
- stream_tenant_index: int32 [256], P(('rep', 'row')), parts along dimension 0, may hold values from 0 to 511, as said below
- live_block_rows: int32 [8], P(('rep', 'row')), parts along dimension 0, may hold values from 1 to 32
Outputs:
- mixed: bfloat16 [256, 2, 8192], P(('rep', 'row'), None, 'head'), parts along dimension 0
- new_state: bfloat16 [256, 64, 64, 128], P(('rep', 'row'), 'head'), parts along dimension 0
There are 2 independent parts, one for each index of `rep`. A program takes and returns all parts, laid end to end along the dimension named above; an argument that names none is the same for every part. Nothing has to cross between parts.
Inputs may be any that keep to these rules, and one draw needn't show every extreme that they name: `stream_tenant_index`: a stream of block b has a tenant of b * 128 up to (b + 1) * 128 - 1.
All inputs are finite; a program needn't handle non-finite values.
Results may differ from a plain program's by a relative error of at most 0.02.
Values may be sent and summed in bfloat16 or wider, within the bound.
A program may use at most 128 MiB of HBM per device.

v0:
```python
import jax
import jax.numpy as jnp
from jax import lax
from jax.sharding import PartitionSpec as P

MODEL_WIDTH = 8192
INNER_WIDTH = 4096


def on_device(
    hidden,
    input_norm_scale,
    projection_signal,
    projection_gate,
    projection_step,
    projection_input_output,
    step_bias,
    head_decay_rate,
    head_skip_weight,
    gated_norm_scale,
    adapter_down_weight,
    adapter_up_weight,
    output_weight,
    scan_state,
    stream_tenant_index,
    live_block_rows,
):
    epsilon = 1e-05
    streams = hidden.shape[0]
    positions = hidden.shape[1]
    inner = projection_signal.shape[1]
    heads_here = projection_step.shape[1]
    state_width = projection_input_output.shape[1] // 2
    feature_width = hidden.shape[2]
    wide = hidden.astype(jnp.float32)
    tenant_local = stream_tenant_index - lax.axis_index("row") * adapter_down_weight.shape[0]
    scaled = (wide * input_norm_scale).astype(jnp.bfloat16)
    down_weight_rows = jnp.take(adapter_down_weight, tenant_local, axis=0)
    square_part = jnp.sum(wide * wide, -1)
    lowrank_part = jnp.einsum(
        "spd,sdr->spr", scaled, down_weight_rows, preferred_element_type=jnp.float32
    )
    squares, lowrank_sum = lax.psum((square_part, lowrank_part), "head")
    inverse = lax.rsqrt(squares / MODEL_WIDTH + epsilon)
    lowrank = (lowrank_sum * inverse[..., None]).astype(jnp.bfloat16)
    normed = (wide * input_norm_scale * inverse[..., None]).astype(jnp.bfloat16)
    features = lax.all_gather(normed, "head", axis=2, tiled=True)
    weight_cat = jnp.concatenate(
        [projection_signal, projection_gate, projection_step, projection_input_output], axis=1
    )
    moved = lax.all_to_all(features, "row", split_axis=2, concat_axis=0, tiled=True)
    moved_flat = moved.reshape(-1, moved.shape[2])
    projected = lax.psum_scatter(
        jnp.dot(moved_flat, weight_cat, preferred_element_type=jnp.float32).astype(jnp.bfloat16),
        "row",
        scatter_dimension=0,
        tiled=True,
    ).astype(jnp.float32)
    projected = projected.reshape(streams, positions, -1)
    xin = projected[..., :inner]
    zin = projected[..., inner : 2 * inner]
    dtin = projected[..., 2 * inner : 2 * inner + heads_here]
    bcin = projected[..., 2 * inner + heads_here :]
    up_weight_rows = jnp.take(adapter_up_weight, tenant_local, axis=0)
    signal = jax.nn.silu(
        xin
        + jnp.einsum("spr,srk->spk", lowrank, up_weight_rows, preferred_element_type=jnp.float32)
    )
    bgate = jax.nn.silu(bcin[..., :state_width])
    cgate = jax.nn.silu(bcin[..., state_width:])
    steps_dt = jax.nn.softplus(dtin + step_bias)
    decay = jnp.exp(-steps_dt * head_decay_rate)
    live = jnp.arange(streams) < live_block_rows[0]
    signal_heads = signal.reshape(streams, positions, heads_here, -1)
    carried = scan_state.astype(jnp.float32)
    outputs = []
    for position in range(positions):
        updated = (
            carried * decay[:, position, :, None, None]
            + (steps_dt[:, position, :, None] * signal_heads[:, position])[..., None]
            * bgate[:, position, None, None, :]
        )
        carried = jnp.where(live[:, None, None, None], updated, carried)
        outputs.append(
            jnp.sum(carried * cgate[:, position, None, None, :], -1)
            + head_skip_weight[None, :, None] * signal_heads[:, position]
        )
    new_state = carried.astype(jnp.bfloat16)
    result = jnp.stack(outputs, 1).reshape(streams, positions, inner)
    gated = result * jax.nn.silu(zin)
    gate_squares = lax.psum(jnp.sum(gated * gated, -1), "head")
    outnorm = (
        gated * lax.rsqrt(gate_squares / INNER_WIDTH + epsilon)[..., None] * gated_norm_scale
    ).astype(jnp.bfloat16)
    out_flat = outnorm.reshape(streams * positions, inner)
    partial_out = jnp.dot(out_flat, output_weight, preferred_element_type=jnp.float32)
    mixer = lax.psum_scatter(
        partial_out.astype(jnp.bfloat16), "head", scatter_dimension=1, tiled=True
    ).astype(jnp.float32)
    mixer = mixer.reshape(streams, positions, feature_width)
    mixed = (wide + jnp.where(live[:, None, None], mixer, 0.0)).astype(jnp.bfloat16)
    return (mixed, new_state)


def solution(mesh):
    in_specs = (
        P(("rep", "row"), None, "head"),
        P("head"),
        P("row", "head"),
        P("row", "head"),
        P("row", "head"),
        P("row", None),
        P("head"),
        P("head"),
        P("head"),
        P("head"),
        P("row", "head", None),
        P("row", None, "head"),
        P("head", None),
        P(("rep", "row"), "head", None, None),
        P(("rep", "row")),
        P(("rep", "row")),
    )
    out_specs = (P(("rep", "row"), None, "head"), P(("rep", "row"), "head", None, None))
    return jax.shard_map(
        on_device, mesh=mesh, in_specs=in_specs, out_specs=out_specs, check_vma=False
    )
```

profile of v0, /device:TPU:0, one launch (start us, length us, event | category | flops | bytes accessed | tf_op | source)
XLA Modules:
  0.0 219.4 jit_solution(15513517323388367327)
XLA Ops:
  7.2 0.7 compare_and_fusion
  7.9 4.1 %gather_fusion = bf16[32,2048,16]{1,2,0:T(8,128)(2,1)S(1)} fusion(bf16[128,2048,16]{1,2,0:T(8,128)(2,1)} %param.26, s32[1024]{0:T(1024)S(1)} %pad_clamp_fusion), kind=kCustom, calls=%fused_computation | custom fusion | bytes 4194432 | tf_op jit(solution)/shard_map/jit(_take)/gather | solution.py:38
  12.2 1.0 fusion.2
  13.3 13.8 %all-reduce = (f32[32,2]{0,1:T(2,128)S(1)}, f32[32,2,16]{2,1,0:T(2,128)}) all-reduce(f32[32,2]{0,1:T(2,128)S(1)} %get-tuple-element.32, f32[32,2,16]{2,1,0:T(2,128)S(1)} %fusion.2), channel_id=1, replica_groups=mesh['rep'=2,'head'=4,'row'=4] {'head'}, use_global_device_ids=true, to_apply=%region_1.2 | all-reduce | flops 1088 | bytes 8704 | tf_op jit(solution)/shard_map/psum | solution.py:43
  27.0 0.8 fusion.10
  27.9 17.2 %all-gather.2.cloned.1.call-done = bf16[32,2,8192]{2,0,1:T(8,128)(2,1)} async-done(((bf16[32,2,2048]{2,0,1:T(8,128)(2,1)}), bf16[32,2,8192]{2,0,1:T(8,128)(2,1)}) %all-gather.2.cloned.1.call-update) | async-done | bytes 1048592 | tf_op jit(solution)/shard_map/all_gather | solution.py:47
  45.0 9.2 %copy.76 = bf16[32,2,8192]{0,1,2:T(2,128)(2,1)} copy(bf16[32,2,8192]{2,0,1:T(8,128)(2,1)} %all-gather.2.cloned.1.call-done) | data formatting | bytes 2097152 | tf_op jit(solution)/shard_map/all_gather | solution.py:47
  54.2 6.4 %reshape.98 = bf16[4,2,65536]{2,1,0:T(2,128)(2,1)} reshape(bf16[8192,2,32]{2,1,0:T(2,128)(2,1)} %bitcast.34) | data formatting | bytes 2097152
  60.6 4.6 %all-to-all-start = ((bf16[4,2,65536]{2,1,0:T(2,128)(2,1)}), bf16[4,2,65536]{2,1,0:T(2,128)(2,1)S(1)}, u32[]{:S(2)}, u32[]{:S(2)}) async-start(bf16[4,2,65536]{2,1,0:T(2,128)(2,1)} %reshape.98), calls=%async_computation | async-start | bytes 2097152 | tf_op jit(solution)/shard_map/all_to_all | solution.py:51
  65.5 15.0 %concatenate.4 = bf16[2048,2320]{1,0:T(8,128)(2,1)} concatenate(bf16[2048,1024]{1,0:T(8,128)(2,1)} %param.18, bf16[2048,1024]{1,0:T(8,128)(2,1)} %param.19, bf16[2048,16]{1,0:T(8,128)(2,1)S(1)} %copy.78, bf16[2048,256]{1,0:T(8,128)(2,1)S(1)} %copy-done.1), dimensions={1} | concatenate | bytes 19005440 | tf_op jit(solution)/shard_map/concatenate | solution.py:48
  80.5 10.8 %all-to-all-done = bf16[4,2,65536]{2,1,0:T(2,128)(2,1)S(1)} async-done(((bf16[4,2,65536]{2,1,0:T(2,128)(2,1)}), bf16[4,2,65536]{2,1,0:T(2,128)(2,1)S(1)}, u32[]{:S(2)}, u32[]{:S(2)}) %all-to-all-start) | async-done | bytes 1048608 | tf_op jit(solution)/shard_map/all_to_all | solution.py:51
  91.3 3.5 %reshape.99 = bf16[8192,2,32]{2,1,0:T(2,128)(2,1)} reshape(bf16[4,2,65536]{2,1,0:T(2,128)(2,1)S(1)} %all-to-all-done) | data formatting | bytes 2097152
  94.7 9.7 %copy.77 = bf16[32,2,4,2048]{3,1,0,2:T(2,128)(2,1)S(1)} copy(bf16[32,2,4,2048]{0,1,3,2:T(2,128)(2,1)} %bitcast.35) | data formatting | bytes 2097152 | tf_op jit(solution)/shard_map/all_to_all | solution.py:51
  104.9 7.7 %convolution_convert_fusion.1 = bf16[256,2320]{1,0:T(8,128)(2,1)} fusion(bf16[256,2048]{1,0:T(8,128)(2,1)S(1)} %reshape.69, bf16[2048,2320]{1,0:T(8,128)(2,1)} %concatenate.4), kind=kOutput, calls=%fused_computation.10 | convolution fusion | flops 2433290240 | bytes 11739136 | tf_op jit(solution)/shard_map/dot_general | solution.py:54
  112.8 2.8 %gather_fusion.1 = bf16[32,16,1024]{2,1,0:T(8,128)(2,1)S(1)} fusion(bf16[128,16,1024]{2,1,0:T(8,128)(2,1)} %param.27, s32[1024]{0:T(1024)S(1)} %pad_clamp_fusion), kind=kCustom, calls=%fused_computation.1 | custom fusion | bytes 2097280 | tf_op jit(solution)/shard_map/jit(_take)/gather | solution.py:64
  116.3 25.0 %reduce-scatter.3.cloned.1.call-done = bf16[64,2320]{1,0:T(8,128)(2,1)} async-done(((bf16[256,2320]{1,0:T(8,128)(2,1)}), bf16[64,2320]{1,0:T(8,128)(2,1)}) %reduce-scatter.3.cloned.1.call-update) | async-done | bytes 296976 | tf_op jit(solution)/shard_map/reduce_scatter | solution.py:53
  141.3 1.3 reshape.77
  144.4 24.9 %multiply_reduce_fusion.1 = (f32[32,16,64]{2,1,0:T(8,128)S(1)}, f32[32,16,64]{2,1,0:T(8,128)S(1)}, bf16[32,16,64,128]{3,2,1,0:T(8,128)(2,1)}) fusion(bf16[32,16,64,128]{3,2,1,0:T(8,128)(2,1)} %param.29, f32[32,128]{1,0:T(8,128)S(1)} %bitcast.39, f32[32,128]{1,0:T(8,128)S(1)} %bitcast.38, f32[32,16,64]{2,1,0:T(8,128)S(1)} %get-tuple-element.30, ...), kind=kLoop, calls=%fused_computation.7 | loop fusion | flops 58654720 | bytes 17371168 | tf_op jit(solution)/shard_map/reduce_sum | solution.py:85
  169.8 0.6 multiply_reduce_fusion.2
  170.4 6.3 %psum.23 = f32[32,2]{0,1:T(2,128)S(1)} all-reduce(f32[32,2]{0,1:T(2,128)S(1)} %copy.86), channel_id=1, replica_groups=mesh['rep'=2,'head'=4,'row'=4] {'head'}, use_global_device_ids=true, to_apply=%region_7.8 | all-reduce | flops 64 | bytes 512 | tf_op jit(solution)/shard_map/psum | solution.py:91
  177.1 9.8 %convolution_convert_fusion = bf16[64,8192]{1,0:T(8,128)(2,1)} fusion(bf16[64,1024]{1,0:T(8,128)(2,1)S(1)} %reshape.73, bf16[1024,8192]{1,0:T(8,128)(2,1)} %param.28), kind=kOutput, calls=%fused_computation.9 | convolution fusion | flops 1074266112 | bytes 17956864 | tf_op jit(solution)/shard_map/dot_general | solution.py:96
  186.9 23.3 %reduce-scatter.5.cloned.1.call-done = bf16[64,2048]{1,0:T(8,128)(2,1)} async-done(((bf16[64,8192]{1,0:T(8,128)(2,1)}), bf16[64,2048]{1,0:T(8,128)(2,1)}) %reduce-scatter.5.cloned.1.call-update) | async-done | bytes 262160 | tf_op jit(solution)/shard_map/reduce_scatter | solution.py:97
  210.3 1.3 reshape.79
  211.9 1.0 copy.89
  (53 shorter events, 4.2 us)
Async XLA Ops:
  7.2 37.9 %all-gather.2.cloned.1.call-start = ((), (), s32[]{:S(2)}) async-start(), calls=%async_computation.3 | async-start | bytes 1310720 | tf_op jit(solution)/shard_map/all_gather | solution.py:47
  7.9 4.1 %copy-start = (bf16[32,2,2048]{2,1,0:T(2,128)(2,1)S(1)}, bf16[32,2,2048]{2,1,0:T(2,128)(2,1)}, u32[]{:S(2)}) copy-start(bf16[32,2,2048]{2,1,0:T(2,128)(2,1)} %param.16) | copy-start | bytes 786436
  7.9 4.1 %copy-start.3 = (f32[2048]{0:T(1024)S(1)}, f32[2048]{0:T(1024)}, u32[]{:S(2)}) copy-start(f32[2048]{0:T(1024)} %param.17) | copy-start | bytes 24580
  12.0 53.1 %copy-start.2 = (bf16[2048,16]{0,1:T(8,128)(2,1)S(1)}, bf16[2048,16]{0,1:T(8,128)(2,1)}, u32[]{:S(2)}) copy-start(bf16[2048,16]{0,1:T(8,128)(2,1)} %param.20) | copy-start | bytes 196612
  12.1 53.4 %copy-start.1 = (bf16[2048,256]{1,0:T(8,128)(2,1)S(1)}, bf16[2048,256]{1,0:T(8,128)(2,1)}, u32[]{:S(2)}) copy-start(bf16[2048,256]{1,0:T(8,128)(2,1)} %param.21) | copy-start | bytes 3145732
  60.6 30.7 %all-to-all-start = ((bf16[4,2,65536]{2,1,0:T(2,128)(2,1)}), bf16[4,2,65536]{2,1,0:T(2,128)(2,1)S(1)}, u32[]{:S(2)}, u32[]{:S(2)}) async-start(bf16[4,2,65536]{2,1,0:T(2,128)(2,1)} %reshape.98), calls=%async_computation | async-start | bytes 2097152 | tf_op jit(solution)/shard_map/all_to_all | solution.py:51
  65.2 76.1 %reduce-scatter.3.cloned.1.call-start = ((), (), s32[]{:S(2)}) async-start(), calls=%async_computation.4 | async-start | bytes 1556480 | tf_op jit(solution)/shard_map/reduce_scatter | solution.py:53
  104.9 37.9 %copy-start.8 = (f32[32,2,16]{2,1,0:T(2,128)S(1)}, f32[32,2,16]{2,1,0:T(2,128)}, u32[]{:S(2)}) copy-start(f32[32,2,16]{2,1,0:T(2,128)} %get-tuple-element.17) | copy-start | bytes 12292
  112.6 31.0 %copy-start.5 = (f32[16]{0:T(128)S(1)}, f32[16]{0:T(128)}, u32[]{:S(2)}) copy-start(f32[16]{0:T(128)} %param.23) | copy-start | bytes 196
  112.6 31.0 %copy-start.6 = (f32[16]{0:T(128)S(1)}, f32[16]{0:T(128)}, u32[]{:S(2)}) copy-start(f32[16]{0:T(128)} %param.22) | copy-start | bytes 196
  112.7 97.6 %reduce-scatter.5.cloned.1.call-start = ((), (), s32[]{:S(2)}) async-start(), calls=%async_computation.5 | async-start | bytes 1310720 | tf_op jit(solution)/shard_map/reduce_scatter | solution.py:97
  143.3 26.0 %copy-start.7 = (f32[16]{0:T(128)S(1)}, f32[16]{0:T(128)}, u32[]{:S(2)}) copy-start(f32[16]{0:T(128)} %param.24) | copy-start | bytes 196
  144.4 32.5 %copy-start.4 = (f32[1024]{0:T(1024)S(1)}, f32[1024]{0:T(1024)}, u32[]{:S(2)}) copy-start(f32[1024]{0:T(1024)} %param.25) | copy-start | bytes 12292
Sparse Core Ops, SparseCore 0:
  28.0 17.0 all-gather.1
  112.8 28.4 reduce-scatter.2
  187.0 23.1 reduce-scatter.4
where the time goes:
time: 221 us; the launch traced here: 219 us
  waiting for transfers between devices  76.4 us (35%)
  local copies, waits for them, and re-layouts  56.3 us (25%)
  other arithmetic  28.3 us (13%)
  blocking collectives  20.1 us (9%)
  matrix products  19 us (9%)
  between operations  14.6 us (7%)
  starting transfers between devices  4.68 us (2%)
    reduce_scatter x1, waiting for transfers between devices, on_device(): lax.psum_scatter(jnp.dot(moved_flat, weight_cat, preferred_element_type=j...  25 us
    reduce_sum x1, other arithmetic, on_device(): jnp.sum(carried * cgate[:, position, None, None, :], -1)  24.9 us
    reduce_scatter x1, waiting for transfers between devices, on_device(): lax.psum_scatter(partial_out.astype(jnp.bfloat16), 'head', scatter_dimens...  23.3 us
    all_gather x1, waiting for transfers between devices, on_device(): features = lax.all_gather(normed, 'head', axis=2, tiled=True)  17.2 us
    concatenate x1, local copies, waits for them, and re-layouts, on_device(): jnp.concatenate([projection_signal, projection_gate, projection_step, pro...  15 us
    psum x1, blocking collectives, on_device(): squares, lowrank_sum = lax.psum((square_part, lowrank_part), 'head')  13.8 us
    unnamed x23, local copies, waits for them, and re-layouts  11.2 us
    all_to_all x1, waiting for transfers between devices, on_device(): lax.all_to_all(features, 'row', split_axis=2, concat_axis=0, tiled=True)  10.8 us
  transfers between devices with their start and end apart: 4, of which 4 were waited for; matrix products, arithmetic and copies ran while one was open for 8% of the time, Pallas kernels for 0%

commit v1 on v0

v1 whole, which is shorter than its diff:
```python
import functools

import jax
import jax.numpy as jnp
from jax import lax
from jax.experimental import pallas as pl
from jax.experimental.pallas import tpu as pltpu
from jax.sharding import PartitionSpec as P

EPSILON = 1e-05
GROUP = 4
BF16 = jnp.bfloat16
F32 = jnp.float32
MESH = pl.DeviceIdType.MESH
LIMIT = 48 * 1024 * 1024
ANY = pl.BlockSpec(memory_space=pl.ANY)
VM = pl.BlockSpec(memory_space=pltpu.VMEM)
SM = pl.BlockSpec(memory_space=pltpu.SMEM)


def nt(a, b):
    return lax.dot_general(a, b, (((1,), (1,)), ((), ())), preferred_element_type=F32)


def split2(a):
    high = a.astype(BF16)
    return high, (a - high.astype(F32)).astype(BF16)


def front_kernel(index_ref, hidden_ref, scale_ref, *rest):
    downs, (scaled_ref, stats_ref) = rest[:GROUP], rest[GROUP:]
    rank = downs[0].shape[1]
    wide = hidden_ref[...].astype(F32)
    scaled = (wide * scale_ref[...]).astype(BF16)
    scaled_ref[...] = scaled
    rows = scaled.shape[0]
    positions = rows // GROUP
    squares = jnp.sum(wide * wide, -1, keepdims=True)
    stack = jnp.concatenate([d[0] for d in downs], axis=0)
    low = nt(scaled, stack)
    row = lax.broadcasted_iota(jnp.int32, low.shape, 0) // positions
    col = lax.broadcasted_iota(jnp.int32, low.shape, 1) // rank
    low = jnp.where(row == col, low, 0.0)
    filler = stats_ref.shape[1] - low.shape[1]
    stats_ref[...] = jnp.concatenate([low, jnp.broadcast_to(squares, (rows, filler))], axis=1)


def front(hidden, scale, down, index, positions):
    tokens, width = hidden.shape
    capacity, rank, _ = down.shape
    rows = GROUP * positions

    def down_spec(j):
        return pl.BlockSpec(
            (1, rank, width), lambda g, idx: (lax.rem(idx[g * GROUP + j], capacity), 0, 0)
        )

    return pl.pallas_call(
        front_kernel,
        grid_spec=pltpu.PrefetchScalarGridSpec(
            num_scalar_prefetch=1,
            grid=(tokens // rows,),
            in_specs=[
                pl.BlockSpec((rows, width), lambda g, idx: (g, 0)),
                pl.BlockSpec((1, width), lambda g, idx: (0, 0)),
            ]
            + [down_spec(j) for j in range(GROUP)],
            out_specs=[
                pl.BlockSpec((rows, width), lambda g, idx: (g, 0)),
                pl.BlockSpec((rows, 128), lambda g, idx: (g, 0)),
            ],
        ),
        out_shape=[
            jax.ShapeDtypeStruct((tokens, width), BF16),
            jax.ShapeDtypeStruct((tokens, 128), F32),
        ],
        name="front",
    )(index, hidden, scale.reshape(1, -1), *([down] * GROUP))


def project_kernel(
    heads, rows, model_width, scaled_ref, stats_ref, wsig_ref, wgate_ref, wstep_ref, wbc_ref,
    proj_ref, low_ref,
    wsig, wgate, wstep, wbc, xbuf, pbuf, rbuf, sbuf,
    w_sem, self_sem, send_a, recv_a, send_b, recv_b, send_s, recv_s, send_r, recv_r,
):
    h = lax.axis_index("head")
    r = lax.axis_index("row")
    tokens, width = scaled_ref.shape
    share = heads // rows
    pieces = min(heads, tokens // 16)
    every = heads // pieces
    prow = tokens // pieces
    inner = wsig.shape[1]
    heads_here = wstep.shape[0]
    loads = [
        pltpu.make_async_copy(s, d, w_sem.at[i])
        for i, (s, d) in enumerate(
            [(wbc_ref, wbc), (wstep_ref, wstep), (wsig_ref, wsig), (wgate_ref, wgate)]
        )
    ]
    for load in loads:
        load.start()
    target_row = h // share
    piece = h // every

    def when(condition):
        return (lambda f: f()) if condition is True else pl.when(condition)

    is_owner = True if every == 1 else (lax.rem(h, every) == 0)

    barrier = pltpu.get_barrier_semaphore()
    for d in range(1, heads):
        pl.semaphore_signal(
            barrier, inc=1, device_id={"head": lax.rem(h + d, heads)}, device_id_type=MESH
        )
    for d in range(1, rows):
        pl.semaphore_signal(
            barrier, inc=1, device_id={"row": lax.rem(r + d, rows)}, device_id_type=MESH
        )

    @when(is_owner)
    def _():
        for j in range(share):
            for e in range(rows):
                src_h = r * share + j
                src_r = lax.rem(r + e, rows)
                same = jnp.logical_and(src_h == h, src_r == r)

                @pl.when(jnp.logical_not(same))
                def _():
                    pl.semaphore_signal(
                        barrier, inc=1, device_id={"head": src_h, "row": src_r},
                        device_id_type=MESH,
                    )

    to_self = jnp.logical_and(lax.rem(h, every) == 0, target_row == r).astype(jnp.int32)
    pl.semaphore_wait(barrier, heads - 1 + rows - 1 + pieces - to_self)

    def a_parts(k):
        src = scaled_ref.at[pl.ds(k * prow, prow), :]
        row0 = pl.multiple_of(r * tokens + k * prow, 16)
        col0 = pl.multiple_of(lax.rem(h, share) * width, 128)
        return src, xbuf.at[pl.ds(row0, prow), pl.ds(col0, width)]

    def a_remote(k):
        src, dst = a_parts(k)
        return pltpu.make_async_remote_copy(
            src_ref=src, dst_ref=dst, send_sem=send_a.at[k],
            recv_sem=recv_a.at[r * share + lax.rem(h, share)],
            device_id={"head": k * every, "row": target_row}, device_id_type=MESH,
        )

    def a_same(k):
        return jnp.logical_and(h == k * every, target_row == r)

    for k in range(pieces):
        @pl.when(jnp.logical_not(a_same(k)))
        def _():
            a_remote(k).start()

        @pl.when(a_same(k))
        def _():
            src, dst = a_parts(k)
            pltpu.make_async_copy(src, dst, recv_a.at[r * share + lax.rem(h, share)]).start()

    stat_copies = []
    for d in range(1, heads):
        copy = pltpu.make_async_remote_copy(
            src_ref=stats_ref, dst_ref=sbuf.at[d], send_sem=send_s.at[d], recv_sem=recv_s.at[d],
            device_id={"head": lax.rem(h + d, heads)}, device_id_type=MESH,
        )
        copy.start()
        stat_copies.append(copy)

    pbuf[:, 2 * inner + wbc.shape[1] :] = jnp.zeros((rows * tokens, 128), BF16)

    def block_rows(e, k):
        row0 = lax.rem(r + e, rows) * tokens + k * prow
        return xbuf.at[pl.ds(pl.multiple_of(row0, 16), prow), :]

    def b_copy(d, e, k):
        return pltpu.make_async_remote_copy(
            src_ref=block_rows(e, k), dst_ref=block_rows(e, k),
            send_sem=send_b.at[d, e], recv_sem=recv_b.at[d, e],
            device_id={"head": lax.rem(h + d, heads)}, device_id_type=MESH,
        )

    @when(is_owner)
    def _():
        for e in range(rows):
            src_r = lax.rem(r + e, rows)
            for j in range(share):
                dst = xbuf.at[
                    pl.ds(pl.multiple_of(src_r * tokens + piece * prow, 16), prow),
                    pl.ds(j * width, width),
                ]
                pltpu.make_async_copy(dst, dst, recv_a.at[src_r * share + j]).wait()
            for d in range(1, heads):
                b_copy(d, e, piece).start()

    for e in range(rows):
        for d in range(1, heads):
            from_h = lax.rem(h - d + heads, heads)

            @when(True if every == 1 else lax.rem(from_h, every) == 0)
            def _():
                b_copy(d, e, from_h // every).wait_recv()

    bc_width = wbc.shape[1]
    half = min(inner, 512)
    chunks = [(wbc, 0, bc_width, 2 * inner, 0), (wstep, None, 128, 2 * inner + bc_width, 1)]
    for i, w in ((2, wsig), (3, wgate)):
        for c in range(0, inner, half):
            chunks.append((w, c, half, (i - 2) * inner + c, i))
    r_copies = []
    waited = set()
    for n, (w, c, cw, out, load) in enumerate(chunks):
        if load not in waited:
            loads[load].wait()
            waited.add(load)
        if c is None:
            pbuf[:, out : out + heads_here] = nt(xbuf[...], w[...]).astype(BF16)
        else:
            pbuf[:, out : out + cw] = jnp.dot(
                xbuf[...], w[:, c : c + cw], preferred_element_type=F32
            ).astype(BF16)
        for d in range(1, rows):
            to = lax.rem(r + d, rows)
            copy = pltpu.make_async_remote_copy(
                src_ref=pbuf.at[pl.ds(pl.multiple_of(to * tokens, 16), tokens), out : out + cw],
                dst_ref=rbuf.at[d, :, out : out + cw],
                send_sem=send_r.at[d, n], recv_sem=recv_r.at[d, n],
                device_id={"row": to}, device_id_type=MESH,
            )
            copy.start()
            r_copies.append((n, copy))

    total = stats_ref[...]
    for d in range(1, heads):
        stat_copies[d - 1].wait_recv()
        total = total + sbuf[d]
    inverse = lax.rsqrt(total[:, 127:128] / model_width + EPSILON)
    low_ref[...] = total * inverse
    own = pl.ds(pl.multiple_of(r * tokens, 16), tokens)
    for n, (w, c, cw, out, load) in enumerate(chunks):
        for m, copy in r_copies:
            if m == n:
                copy.wait_recv()
        part = pbuf[own, out : out + cw].astype(F32)
        for d in range(1, rows):
            part = part + rbuf[d, :, out : out + cw].astype(F32)
        proj_ref[:, out : out + cw] = part * inverse

    for _, copy in r_copies:
        copy.wait_send()
    for copy in stat_copies:
        copy.wait_send()
    for k in range(pieces):
        @pl.when(jnp.logical_not(a_same(k)))
        def _():
            a_remote(k).wait_send()

    @when(is_owner)
    def _():
        for e in range(rows):
            for d in range(1, heads):
                b_copy(d, e, piece).wait_send()


def project(scaled, stats, wsig, wgate, wstep, wbc, heads, rows):
    tokens, width = scaled.shape
    depth, inner = wsig.shape
    out_width = 2 * inner + wbc.shape[1] + 128
    share = heads // rows
    pieces = min(heads, tokens // 16)
    n_chunks = 2 + 2 * (inner // min(inner, 512))
    dma = pltpu.SemaphoreType.DMA
    return pl.pallas_call(
        functools.partial(project_kernel, heads, rows, float(width * heads)),
        out_shape=[
            jax.ShapeDtypeStruct((tokens, out_width), F32),
            jax.ShapeDtypeStruct((tokens, 128), F32),
        ],
        in_specs=[VM, VM, ANY, ANY, ANY, ANY],
        out_specs=[VM, VM],
        scratch_shapes=[
            pltpu.VMEM(wsig.shape, BF16),
            pltpu.VMEM(wgate.shape, BF16),
            pltpu.VMEM(wstep.shape, BF16),
            pltpu.VMEM(wbc.shape, BF16),
            pltpu.VMEM((rows * tokens, depth), BF16),
            pltpu.VMEM((rows * tokens, out_width), BF16),
            pltpu.VMEM((rows, tokens, out_width), BF16),
            pltpu.VMEM((heads, tokens, 128), F32),
            dma((4,)),
            dma((1,)),
            dma((pieces,)),
            dma((rows * share,)),
            dma((heads, rows)),
            dma((heads, rows)),
            dma((heads,)),
            dma((heads,)),
            dma((rows, n_chunks)),
            dma((rows, n_chunks)),
        ],
        compiler_params=pltpu.CompilerParams(
            collective_id=0, has_side_effects=True, vmem_limit_bytes=LIMIT
        ),
        name="project",
    )(scaled, stats, wsig, wgate, wstep, wbc)


def scan_kernel(
    positions, index_ref, live_ref, proj_ref, low_ref, bias_ref, rate_ref, skip_ref, gain_ref,
    spread_ref, state_ref, *rest
):
    ups, (new_ref, gated_ref, sq_ref) = rest[:GROUP], rest[GROUP:]
    g = pl.program_id(0)
    rows = proj_ref.shape[0]
    inner = ups[0].shape[2]
    rank = ups[0].shape[1]
    n_state = state_ref.shape[3]
    shape_state = state_ref.shape[1:]
    base = 2 * inner
    xin = proj_ref[:, :inner]
    zin = proj_ref[:, inner:base]
    bc = proj_ref[:, base : base + 2 * n_state]
    dtin = proj_ref[:, base + 2 * n_state :]
    low = low_ref[:, : GROUP * rank].astype(BF16)
    up = jnp.concatenate([u[0] for u in ups], axis=0)
    x = jax.nn.silu(xin + jnp.dot(low, up, preferred_element_type=F32))
    bgate = jax.nn.silu(bc[:, :n_state])
    cgate = jax.nn.silu(bc[:, n_state:])
    row1 = lax.broadcasted_iota(jnp.int32, (rows, 1), 0)
    stream1 = row1 // positions
    live = (g * GROUP + stream1) < live_ref[0]
    dt = jax.nn.softplus(dtin + bias_ref[...])
    decay = jnp.exp(-dt * rate_ref[...])
    dt_high, dt_low = split2(dt)
    de_high, de_low = split2(decay)
    spread = jnp.dot(
        jnp.concatenate([dt_high, dt_low, de_high, de_low], axis=0), spread_ref[...],
        preferred_element_type=F32,
    )
    dt_wide = spread[:rows] + spread[rows : 2 * rows]
    de_wide = spread[2 * rows : 3 * rows] + spread[3 * rows :]
    u = jnp.where(live, dt_wide * x, 0.0)
    de_wide = jnp.where(live, de_wide, 1.0)

    second = lax.rem(row1, positions) == 1
    prev_de = pltpu.roll(de_wide, 1, 0)
    prev_u = pltpu.roll(u, 1, 0)
    prev_b = pltpu.roll(bgate, 1, 0)
    keep = jnp.where(second, de_wide * prev_de, de_wide)
    carried_u = jnp.where(second, u, u * pltpu.roll(de_wide, rows - 1, 0))
    keep_high, keep_low = split2(keep)
    left = jnp.concatenate(
        [carried_u.astype(BF16), keep_high, keep_low, jnp.zeros_like(keep_low)], axis=0
    )
    left = left.T
    y = jnp.zeros((rows, inner), F32)
    zero_b = jnp.zeros((rows, n_state), F32)
    for j in range(GROUP):
        mine = stream1 == j
        b_mine = jnp.where(mine, bgate, 0.0)
        ones_mine = jnp.broadcast_to(jnp.where(mine & second, 1.0, 0.0), (rows, n_state))
        right = jnp.concatenate(
            [
                jnp.concatenate([b_mine, zero_b], axis=1),
                jnp.concatenate([zero_b, ones_mine], axis=1),
                jnp.concatenate([zero_b, ones_mine], axis=1),
                jnp.concatenate([zero_b, zero_b], axis=1),
            ],
            axis=0,
        ).astype(BF16)
        state = state_ref[j].reshape(inner, n_state)
        both = jnp.dot(left, right, preferred_element_type=F32)
        new = state.astype(F32) * both[:, n_state:] + both[:, :n_state]
        new_ref[j] = new.astype(BF16).reshape(shape_state)
        y = y + nt(jnp.where(mine, cgate, 0.0).astype(BF16), state)

    dot_own = jnp.sum(bgate * cgate, -1, keepdims=True)
    dot_prev = jnp.sum(prev_b * cgate, -1, keepdims=True)
    y = keep * y + u * dot_own + jnp.where(second, de_wide * prev_u * dot_prev, 0.0)
    y = y + skip_ref[...] * x
    gated = y * jax.nn.silu(zin)
    gated_ref[...] = (gated * gain_ref[...]).astype(BF16)
    sq_ref[...] = jnp.broadcast_to(jnp.sum(gated * gated, -1, keepdims=True), sq_ref.shape)


def scan(index, live, proj, low, bias, rate, skip, gain, state, up, positions):
    tokens, out_width = proj.shape
    capacity, rank, inner = up.shape
    rows = GROUP * positions
    heads_here = bias.shape[0]
    head_size = inner // heads_here
    spread = (jnp.arange(128)[:, None] == jnp.arange(inner)[None, :] // head_size).astype(BF16)
    pad = ((0, 0), (0, 128 - heads_here))
    bias = jnp.pad(bias.reshape(1, -1), pad)
    rate = jnp.pad(rate.reshape(1, -1), pad)
    skip = jnp.repeat(skip, head_size).reshape(1, -1)

    def up_spec(j):
        return pl.BlockSpec(
            (1, rank, inner), lambda g, idx, lv: (lax.rem(idx[g * GROUP + j], capacity), 0, 0)
        )

    def whole(a):
        return pl.BlockSpec(a.shape, lambda g, idx, lv: (0, 0))

    def by_rows(w):
        return pl.BlockSpec((rows, w), lambda g, idx, lv: (g, 0))

    gain = gain.reshape(1, -1)
    state_spec = pl.BlockSpec((GROUP,) + state.shape[1:], lambda g, idx, lv: (g, 0, 0, 0))
    return pl.pallas_call(
        functools.partial(scan_kernel, positions),
        grid_spec=pltpu.PrefetchScalarGridSpec(
            num_scalar_prefetch=2,
            grid=(tokens // rows,),
            in_specs=[by_rows(out_width), by_rows(128), whole(bias), whole(rate), whole(skip),
                      whole(gain), whole(spread), state_spec]
            + [up_spec(j) for j in range(GROUP)],
            out_specs=[state_spec, by_rows(inner), by_rows(128)],
        ),
        out_shape=[
            jax.ShapeDtypeStruct(state.shape, BF16),
            jax.ShapeDtypeStruct((tokens, inner), BF16),
            jax.ShapeDtypeStruct((tokens, 128), F32),
        ],
        compiler_params=pltpu.CompilerParams(vmem_limit_bytes=LIMIT),
        name="scan",
    )(index, live, proj, low, bias, rate, skip, gain, spread, state, *([up] * GROUP))


def output_kernel(
    heads, positions, inner_width, live_ref, gated_ref, sq_ref, hidden_ref, w_ref, out_ref,
    wbuf, pbuf, rbuf, sbuf, w_sem, send_s, recv_s, send_r, recv_r,
):
    h = lax.axis_index("head")
    tokens, width = hidden_ref.shape
    order = [d for d in range(1, heads)] + [0]
    order = sorted(order, key=lambda d: (d == 0, abs(d - heads // 2)))

    def load(d):
        to = lax.rem(h + d, heads)
        return pltpu.make_async_copy(
            w_ref.at[:, pl.ds(pl.multiple_of(to * width, 128), width)], wbuf.at[d], w_sem.at[d]
        )

    for d in order:
        load(d).start()
    barrier = pltpu.get_barrier_semaphore()
    for d in range(1, heads):
        pl.semaphore_signal(
            barrier, inc=1, device_id={"head": lax.rem(h + d, heads)}, device_id_type=MESH
        )
    pl.semaphore_wait(barrier, heads - 1)
    copies = []
    for d in range(1, heads):
        copy = pltpu.make_async_remote_copy(
            src_ref=sq_ref, dst_ref=sbuf.at[d], send_sem=send_s.at[d], recv_sem=recv_s.at[d],
            device_id={"head": lax.rem(h + d, heads)}, device_id_type=MESH,
        )
        copy.start()
        copies.append(copy)
    parts = {}
    step = min(width, 512)
    for d in order:
        load(d).wait()
        for c in range(0, width, step):
            pbuf[d, :, c : c + step] = jnp.dot(
                gated_ref[...], wbuf[d, :, c : c + step], preferred_element_type=F32
            ).astype(BF16)
        if d:
            copy = pltpu.make_async_remote_copy(
                src_ref=pbuf.at[d], dst_ref=rbuf.at[d], send_sem=send_r.at[d],
                recv_sem=recv_r.at[d],
                device_id={"head": lax.rem(h + d, heads)}, device_id_type=MESH,
            )
            copy.start()
            parts[d] = copy
    square = sq_ref[...]
    for d in range(1, heads):
        copies[d - 1].wait_recv()
        square = square + sbuf[d]
    inverse = lax.rsqrt(square[:, :1] / inner_width + EPSILON)
    mixer = pbuf[0].astype(F32)
    for d in sorted(parts, key=lambda d: -abs(d - heads // 2)):
        parts[d].wait_recv()
        mixer = mixer + rbuf[d].astype(F32)
    stream = lax.broadcasted_iota(jnp.int32, (tokens, 1), 0) // positions
    live = stream < live_ref[0]
    out_ref[...] = (
        hidden_ref[...].astype(F32) + jnp.where(live, mixer * inverse, 0.0)
    ).astype(BF16)
    for copy in copies:
        copy.wait_send()
    for copy in parts.values():
        copy.wait_send()


def output(live, gated, sq, hidden, weight, heads, positions):
    tokens, width = hidden.shape
    inner = gated.shape[1]
    dma = pltpu.SemaphoreType.DMA
    return pl.pallas_call(
        functools.partial(output_kernel, heads, positions, float(inner * heads)),
        out_shape=jax.ShapeDtypeStruct((tokens, width), BF16),
        in_specs=[SM, VM, VM, VM, ANY],
        out_specs=VM,
        scratch_shapes=[
            pltpu.VMEM((heads, inner, width), BF16),
            pltpu.VMEM((heads, tokens, width), BF16),
            pltpu.VMEM((heads, tokens, width), BF16),
            pltpu.VMEM((heads, tokens, 128), F32),
            dma((heads,)),
            dma((heads,)),
            dma((heads,)),
            dma((heads,)),
            dma((heads,)),
        ],
        compiler_params=pltpu.CompilerParams(
            collective_id=1, has_side_effects=True, vmem_limit_bytes=LIMIT
        ),
        name="output",
    )(live, gated, sq, hidden, weight)


def on_device(
    heads, rows,
    hidden, input_norm_scale, projection_signal, projection_gate, projection_step,
    projection_input_output, step_bias, head_decay_rate, head_skip_weight, gated_norm_scale,
    adapter_down_weight, adapter_up_weight, output_weight, scan_state, stream_tenant_index,
    live_block_rows,
):
    streams, positions, width = hidden.shape
    flat = hidden.reshape(streams * positions, width)
    down = jnp.swapaxes(adapter_down_weight, 1, 2)
    scaled, stats = front(flat, input_norm_scale, down, stream_tenant_index, positions)
    proj, low = project(
        scaled, stats, projection_signal, projection_gate, projection_step.T,
        projection_input_output, heads, rows,
    )
    new_state, gated, sq = scan(
        stream_tenant_index, live_block_rows, proj, low, step_bias, head_decay_rate,
        head_skip_weight, gated_norm_scale, scan_state, adapter_up_weight, positions,
    )
    mixed = output(live_block_rows, gated, sq, flat, output_weight, heads, positions)
    return mixed.reshape(hidden.shape), new_state


def solution(mesh):
    in_specs = (
        P(("rep", "row"), None, "head"),
        P("head"),
        P("row", "head"),
        P("row", "head"),
        P("row", "head"),
        P("row", None),
        P("head"),
        P("head"),
        P("head"),
        P("head"),
        P("row", "head", None),
        P("row", None, "head"),
        P("head", None),
        P(("rep", "row"), "head", None, None),
        P(("rep", "row")),
        P(("rep", "row")),
    )
    out_specs = (P(("rep", "row"), None, "head"), P(("rep", "row"), "head", None, None))
    return jax.shard_map(
        functools.partial(on_device, mesh.shape["head"], mesh.shape["row"]),
        mesh=mesh, in_specs=in_specs, out_specs=out_specs, check_vma=False,
    )
```

time: 221 us -> 99.1 us (0.45)
  Pallas kernels: 0 us -> 90.1 us
  waiting for transfers between devices: 76.4 us -> 0 us
  local copies, waits for them, and re-layouts: 56.3 us -> 6.86 us
  other arithmetic: 28.3 us -> 0.06 us
  blocking collectives: 20.1 us -> 0 us
  matrix products: 19 us -> 0 us
  between operations: 14.6 us -> 1.36 us
  starting transfers between devices: 4.68 us -> 0 us
    pallas_call x0 -> x4, Pallas kernels: none -> 90.1 us  [the longest x1 54.5 us: project(): pl.pallas_call(functools.partial(project_kernel, heads, rows, float(width...]
    reduce_scatter x2 -> x0, waiting for transfers between devices: 48.4 us -> none  [the longest x1 25 us: on_device(): lax.psum_scatter(jnp.dot(moved_flat, weight_cat, preferred_element_type=j...]
    reduce_sum x2 -> x0, other arithmetic: 25.4 us -> none  [the longest x1 24.9 us: on_device(): jnp.sum(carried * cgate[:, position, None, None, :], -1)]
    psum x2 -> x0, blocking collectives: 20.1 us -> none  [the longest x1 13.8 us: on_device(): squares, lowrank_sum = lax.psum((square_part, lowrank_part), 'head')]
    dot_general x4 -> x0, matrix products: 19 us -> none  [the longest x1 9.76 us: on_device(): jnp.dot(out_flat, output_weight, preferred_element_type=jnp.float32)]
    all_gather x1 -> x0, waiting for transfers between devices: 17.2 us -> none  [on_device(): features = lax.all_gather(normed, 'head', axis=2, tiled=True)]
    concatenate x1 -> x0, local copies, waits for them, and re-layouts: 15 us -> none  [on_device(): jnp.concatenate([projection_signal, projection_gate, projection_step, pro...]
    all_to_all x1 -> x0, waiting for transfers between devices: 10.8 us -> none  [on_device(): lax.all_to_all(features, 'row', split_axis=2, concat_axis=0, tiled=True)]
  transfers between devices with their start and end apart: 4 -> 0, of which waited for: 4 -> 0; matrix products, arithmetic and copies ran while one was open for 8% -> 0% of each run, Pallas kernels for 0% -> 0%
where the time goes in v1:
time: 99.1 us; the launch traced here: 98.3 us
  Pallas kernels  90.1 us (91%)
  local copies, waits for them, and re-layouts  6.86 us (7%)
  between operations  1.36 us (1%)
    pallas_call x1, Pallas kernels, project(): pl.pallas_call(functools.partial(project_kernel, heads, rows, float(width...  54.5 us
    pallas_call x1, Pallas kernels, output(): pl.pallas_call(functools.partial(output_kernel, heads, positions, float(i...  15.6 us
    pallas_call x1, Pallas kernels, scan(): pl.pallas_call(functools.partial(scan_kernel, positions), grid_spec=pltpu...  13.4 us
    pallas_call x1, Pallas kernels, front(): pl.pallas_call(front_kernel, grid_spec=pltpu.PrefetchScalarGridSpec(num_s...  6.66 us
    unnamed x16, local copies, waits for them, and re-layouts  2.1 us

profile of v1, /device:TPU:0, one launch (start us, length us, event | category | flops | bytes accessed | tf_op | source)
XLA Modules:
  0.0 98.3 jit_solution(4876146120589777523)
XLA Ops:
  1.3 0.7 pad.7.bias_ref
  1.9 0.7 pad.8.rate_ref
  2.6 0.7 broadcast_in_dim.2
  3.3 0.1 reshape_reshape.3.skip_ref
  3.4 0.1 fusion.spread_ref
  3.5 1.8 %reshape.59.hidden_ref = bf16[64,2048]{1,0:T(8,128)(2,1)} reshape(bf16[32,2,2048]{2,1,0:T(2,128)(2,1)} %param.16) | data formatting | bytes 524288 | tf_op jit(solution)/shard_map/reshape | solution.py:539
  5.2 0.0 copy-start.2
  5.2 0.0 copy-start.4
  5.2 0.0 copy-start.6
  5.2 6.7 %front.1 = (bf16[64,2048]{1,0:T(8,128)(2,1)}, f32[64,128]{1,0:T(8,128)}) custom-call(s32[32]{0:T(128)} %index_ref.3, bf16[64,2048]{1,0:T(8,128)(2,1)} %reshape.59.hidden_ref, f32[1,2048]{1,0:T(1,128)} %bitcast.12, bf16[128,16,2048]{2,1,0:T(8,128)(2,1)} %bitcast.8, bf16[128,16,2048]{2,1,0:T(8,128)(2,1)} %bitcast.9, bf16[128,16,2048]{2,1,0:T(8,128)(2,1)} %bitcast.10, ...), custom_call_target="tpu_custom_call" | custom-call | tf_op jit(solution)/shard_map/front/pallas_call | solution.py:58
  11.9 0.0 copy-done.2
  11.9 0.0 copy-done.4
  11.9 0.0 copy-start.3
  11.9 1.1 %copy-done.3 = bf16[64,2048]{1,0:T(8,128)(2,1)S(1)} copy-done((bf16[64,2048]{1,0:T(8,128)(2,1)S(1)}, bf16[64,2048]{1,0:T(8,128)(2,1)}, u32[]{:S(2)}) %copy-start.3) | copy-done | bytes 262168
  13.0 1.0 copy-done.5
  14.0 54.5 %project.1 = (f32[64,2432]{1,0:T(8,128)S(1)}, f32[64,128]{1,0:T(8,128)S(1)}) custom-call(bf16[64,2048]{1,0:T(8,128)(2,1)S(1)} %copy-done.3, f32[64,128]{1,0:T(8,128)S(1)} %copy-done.5, bf16[2048,1024]{1,0:T(8,128)(2,1)} %wsig_ref.1, bf16[2048,1024]{1,0:T(8,128)(2,1)} %wgate_ref.1, bf16[16,2048]{1,0:T(8,128)(2,1)S(1)} %bitcast.6, bf16[2048,256]{1,0:T(8,128)(2,1)S(1)} %copy-done.2), custom_call_target="tpu_custom_call" | custom-call | tf_op jit(solution)/shard_map/project/pallas_call | solution.py:279
  68.4 0.0 copy-done.6
  68.5 0.0 copy-done.7
  68.5 0.0 copy-done
  68.5 0.0 copy-start.1
  68.5 13.4 %scan.1 = (bf16[32,16,64,128]{3,2,1,0:T(8,128)(2,1)}, bf16[64,1024]{1,0:T(8,128)(2,1)S(1)}, f32[64,128]{1,0:T(8,128)S(1)}) custom-call(s32[32]{0:T(128)S(1)} %copy-done.7, s32[1]{0:T(128)S(6)} %copy.18.live_ref, f32[64,2432]{1,0:T(8,128)S(1)} %get-tuple-element.11.proj_ref, f32[64,128]{1,0:T(8,128)S(1)} %get-tuple-element.12.low_ref, ...), custom_call_target="tpu_custom_call" | custom-call | tf_op jit(solution)/shard_map/scan/pallas_call | solution.py:417
  81.9 0.0 copy-done.1
  81.9 15.6 %output.1 = bf16[64,2048]{1,0:T(8,128)(2,1)S(1)} custom-call(s32[1]{0:T(128)S(6)} %copy.18.live_ref, bf16[64,1024]{1,0:T(8,128)(2,1)S(1)} %get-tuple-element.13.gated_ref, f32[64,128]{1,0:T(8,128)S(1)} %get-tuple-element.14.sq_ref, bf16[64,2048]{1,0:T(8,128)(2,1)S(1)} %copy-done.1, bf16[1024,8192]{1,0:T(8,128)(2,1)} %w_ref.1), custom_call_target="tpu_custom_call" | custom-call | tf_op jit(solution)/shard_map/output/pallas_call | solution.py:508
  97.5 0.9 reshape.64
  (4 shorter events, 0.0 us)
Async XLA Ops:
  5.2 6.7 %copy-start.2 = (bf16[2048,256]{1,0:T(8,128)(2,1)S(1)}, bf16[2048,256]{1,0:T(8,128)(2,1)}, u32[]{:S(2)}) copy-start(bf16[2048,256]{1,0:T(8,128)(2,1)} %wbc_ref.1) | copy-start | bytes 3145732
  5.2 6.7 %copy-start.4 = (bf16[2048,16]{0,1:T(8,128)(2,1)S(1)}, bf16[2048,16]{0,1:T(8,128)(2,1)}, u32[]{:S(2)}) copy-start(bf16[2048,16]{0,1:T(8,128)(2,1)} %param.20) | copy-start | bytes 196612
  5.2 63.2 %copy-start.6 = (f32[1024]{0:T(1024)S(1)}, f32[1024]{0:T(1024)}, u32[]{:S(2)}) copy-start(f32[1024]{0:T(1024)} %param.25) | copy-start | bytes 12292
  5.2 63.2 %copy-start.7 = (s32[32]{0:T(128)S(1)}, s32[32]{0:T(128)}, u32[]{:S(2)}) copy-start(s32[32]{0:T(128)} %index_ref.3) | copy-start | bytes 388
  11.9 56.6 %copy-start = (bf16[128,16,1024]{2,1,0:T(8,128)(2,1)S(1)}, bf16[128,16,1024]{2,1,0:T(8,128)(2,1)}, u32[]{:S(2)}) copy-start(bf16[128,16,1024]{2,1,0:T(8,128)(2,1)} %rest_3_.1) | copy-start | bytes 12582916
  11.9 1.1 %copy-start.3 = (bf16[64,2048]{1,0:T(8,128)(2,1)S(1)}, bf16[64,2048]{1,0:T(8,128)(2,1)}, u32[]{:S(2)}) copy-start(bf16[64,2048]{1,0:T(8,128)(2,1)} %get-tuple-element.9.scaled_ref) | copy-start | bytes 786436
  13.0 1.0 copy-start.5
  68.5 13.4 %copy-start.1 = (bf16[64,2048]{1,0:T(8,128)(2,1)S(1)}, bf16[64,2048]{1,0:T(8,128)(2,1)}, u32[]{:S(2)}) copy-start(bf16[64,2048]{1,0:T(8,128)(2,1)} %reshape.59.hidden_ref) | copy-start | bytes 786436

commit v2 on v1

--- a/solution.py
+++ b/solution.py
@@ -27,62 +27,64 @@
     return high, (a - high.astype(F32)).astype(BF16)
 
 
-def front_kernel(index_ref, hidden_ref, scale_ref, *rest):
-    downs, (scaled_ref, stats_ref) = rest[:GROUP], rest[GROUP:]
-    rank = downs[0].shape[1]
+def front_kernel(
+    capacity, positions, index_ref, hidden_ref, scale_ref, down_ref, scaled_ref, stats_ref,
+    dbuf, sems,
+):
+    tokens = hidden_ref.shape[0]
+    rank = down_ref.shape[1]
+    copies = []
+    for s in range(tokens // positions):
+        copy = pltpu.make_async_copy(
+            down_ref.at[lax.rem(index_ref[s], capacity)],
+            dbuf.at[s * rank : (s + 1) * rank, :], sems.at[s],
+        )
+        copy.start()
+        copies.append(copy)
     wide = hidden_ref[...].astype(F32)
-    scaled = (wide * scale_ref[...]).astype(BF16)
-    scaled_ref[...] = scaled
-    rows = scaled.shape[0]
-    positions = rows // GROUP
+    scaled_ref[...] = (wide * scale_ref[...]).astype(BF16)
     squares = jnp.sum(wide * wide, -1, keepdims=True)
-    stack = jnp.concatenate([d[0] for d in downs], axis=0)
-    low = nt(scaled, stack)
-    row = lax.broadcasted_iota(jnp.int32, low.shape, 0) // positions
-    col = lax.broadcasted_iota(jnp.int32, low.shape, 1) // rank
-    low = jnp.where(row == col, low, 0.0)
-    filler = stats_ref.shape[1] - low.shape[1]
-    stats_ref[...] = jnp.concatenate([low, jnp.broadcast_to(squares, (rows, filler))], axis=1)
+    streams = 2 * GROUP
+    rows = streams * positions
+    lanes = streams * rank
+    row = lax.broadcasted_iota(jnp.int32, (rows, lanes), 0) // positions
+    col = lax.broadcasted_iota(jnp.int32, (rows, lanes), 1) // rank
+    for g in range(tokens // rows):
+        for copy in copies[g * streams : (g + 1) * streams]:
+            copy.wait()
+        here = slice(g * rows, (g + 1) * rows)
+        low = nt(scaled_ref[here, :], dbuf[g * lanes : (g + 1) * lanes, :])
+        low = jnp.where(row < GROUP, low, pltpu.roll(low, lanes // 2, 1))
+        low = jnp.where(lax.rem(row, GROUP) == col, low, 0.0)
+        stats_ref[here, :] = jnp.where(col < GROUP, low, squares[here, :])
 
 
 def front(hidden, scale, down, index, positions):
     tokens, width = hidden.shape
     capacity, rank, _ = down.shape
-    rows = GROUP * positions
-
-    def down_spec(j):
-        return pl.BlockSpec(
-            (1, rank, width), lambda g, idx: (lax.rem(idx[g * GROUP + j], capacity), 0, 0)
-        )
-
+    streams = tokens // positions
     return pl.pallas_call(
-        front_kernel,
-        grid_spec=pltpu.PrefetchScalarGridSpec(
-            num_scalar_prefetch=1,
-            grid=(tokens // rows,),
-            in_specs=[
-                pl.BlockSpec((rows, width), lambda g, idx: (g, 0)),
-                pl.BlockSpec((1, width), lambda g, idx: (0, 0)),
-            ]
-            + [down_spec(j) for j in range(GROUP)],
-            out_specs=[
-                pl.BlockSpec((rows, width), lambda g, idx: (g, 0)),
-                pl.BlockSpec((rows, 128), lambda g, idx: (g, 0)),
-            ],
-        ),
+        functools.partial(front_kernel, capacity, positions),
+        in_specs=[SM, VM, VM, ANY],
+        out_specs=[VM, VM],
         out_shape=[
             jax.ShapeDtypeStruct((tokens, width), BF16),
             jax.ShapeDtypeStruct((tokens, 128), F32),
         ],
+        scratch_shapes=[
+            pltpu.VMEM((streams * rank, width), BF16),
+            pltpu.SemaphoreType.DMA((streams,)),
+        ],
+        compiler_params=pltpu.CompilerParams(vmem_limit_bytes=24 * 1024 * 1024),
         name="front",
-    )(index, hidden, scale.reshape(1, -1), *([down] * GROUP))
+    )(index, hidden, scale.reshape(1, -1), down)
 
 
 def project_kernel(
     heads, rows, model_width, scaled_ref, stats_ref, wsig_ref, wgate_ref, wstep_ref, wbc_ref,
     proj_ref, low_ref,
-    wsig, wgate, wstep, wbc, xbuf, pbuf, rbuf, sbuf,
-    w_sem, self_sem, send_a, recv_a, send_b, recv_b, send_s, recv_s, send_r, recv_r,
+    wsig, wgate, wstep, wbc, xbuf, pbuf, rup, rdown, sbuf,
+    w_sem, send_a, recv_a, send_b, recv_b, send_s, recv_s, send_r, recv_u, recv_d,
 ):
     h = lax.axis_index("head")
     r = lax.axis_index("row")
@@ -213,7 +215,40 @@
     for i, w in ((2, wsig), (3, wgate)):
         for c in range(0, inner, half):
             chunks.append((w, c, half, (i - 2) * inner + c, i))
-    r_copies = []
+
+    def columns(n):
+        return slice(chunks[n][3], chunks[n][3] + chunks[n][2])
+
+    def hop(t, n, up):
+        there = lax.rem(r + (1 if up else rows - 1), rows)
+        return pltpu.make_async_remote_copy(
+            src_ref=pbuf.at[t * tokens : (t + 1) * tokens, columns(n)],
+            dst_ref=(rup if up else rdown).at[t, :, columns(n)],
+            send_sem=send_r.at[t, n], recv_sem=(recv_u if up else recv_d).at[t, n],
+            device_id={"row": there}, device_id_type=MESH,
+        )
+
+    def first_hop(n):
+        @pl.when(r == 0)
+        def _():
+            for t in range(rows - 1, 0, -1):
+                hop(t, n, True).start()
+
+        @pl.when(r == rows - 1)
+        def _():
+            for t in range(rows - 1):
+                hop(t, n, False).start()
+
+    def pass_on(t, n, up):
+        copy = hop(t, n, up)
+        copy.wait_recv()
+        here = slice(t * tokens, (t + 1) * tokens)
+        came = (rup if up else rdown)[t, :, columns(n)]
+        pbuf[here, columns(n)] = (
+            pbuf[here, columns(n)].astype(F32) + came.astype(F32)
+        ).astype(BF16)
+        copy.start()
+
     waited = set()
     for n, (w, c, cw, out, load) in enumerate(chunks):
         if load not in waited:
@@ -225,16 +260,21 @@
             pbuf[:, out : out + cw] = jnp.dot(
                 xbuf[...], w[:, c : c + cw], preferred_element_type=F32
             ).astype(BF16)
-        for d in range(1, rows):
-            to = lax.rem(r + d, rows)
-            copy = pltpu.make_async_remote_copy(
-                src_ref=pbuf.at[pl.ds(pl.multiple_of(to * tokens, 16), tokens), out : out + cw],
-                dst_ref=rbuf.at[d, :, out : out + cw],
-                send_sem=send_r.at[d, n], recv_sem=recv_r.at[d, n],
-                device_id={"row": to}, device_id_type=MESH,
-            )
-            copy.start()
-            r_copies.append((n, copy))
+        first_hop(n)
+
+    for step in range(len(chunks) + rows - 3):
+        for k in range(1, rows - 1):
+            n = step - (k - 1)
+            if 0 <= n < len(chunks):
+                @pl.when(r == k)
+                def _():
+                    for t in range(rows - 1, k, -1):
+                        pass_on(t, n, True)
+
+                @pl.when(r == rows - 1 - k)
+                def _():
+                    for t in range(rows - 1 - k):
+                        pass_on(t, n, False)
 
     total = stats_ref[...]
     for d in range(1, heads):
@@ -243,17 +283,25 @@
     inverse = lax.rsqrt(total[:, 127:128] / model_width + EPSILON)
     low_ref[...] = total * inverse
     own = pl.ds(pl.multiple_of(r * tokens, 16), tokens)
-    for n, (w, c, cw, out, load) in enumerate(chunks):
-        for m, copy in r_copies:
-            if m == n:
-                copy.wait_recv()
-        part = pbuf[own, out : out + cw].astype(F32)
-        for d in range(1, rows):
-            part = part + rbuf[d, :, out : out + cw].astype(F32)
-        proj_ref[:, out : out + cw] = part * inverse
-
-    for _, copy in r_copies:
-        copy.wait_send()
+    for n in range(len(chunks)):
+        proj_ref[:, columns(n)] = pbuf[own, columns(n)].astype(F32)
+        for buffer, sem, there in ((rup, recv_u, r > 0), (rdown, recv_d, r < rows - 1)):
+            @pl.when(there)
+            def _():
+                came = buffer.at[r, :, columns(n)]
+                pltpu.make_async_copy(came, came, sem.at[r, n]).wait()
+                proj_ref[:, columns(n)] = proj_ref[:, columns(n)] + came[...].astype(F32)
+        proj_ref[:, columns(n)] = proj_ref[:, columns(n)] * inverse
+
+    for n in range(len(chunks)):
+        for t in range(rows):
+            @pl.when(t > r)
+            def _():
+                hop(t, n, True).wait_send()
+
+            @pl.when(t < r)
+            def _():
+                hop(t, n, False).wait_send()
     for copy in stat_copies:
         copy.wait_send()
     for k in range(pieces):
@@ -292,15 +340,16 @@
             pltpu.VMEM((rows * tokens, depth), BF16),
             pltpu.VMEM((rows * tokens, out_width), BF16),
             pltpu.VMEM((rows, tokens, out_width), BF16),
+            pltpu.VMEM((rows, tokens, out_width), BF16),
             pltpu.VMEM((heads, tokens, 128), F32),
             dma((4,)),
-            dma((1,)),
             dma((pieces,)),
             dma((rows * share,)),
             dma((heads, rows)),
             dma((heads, rows)),
             dma((heads,)),
             dma((heads,)),
+            dma((rows, n_chunks)),
             dma((rows, n_chunks)),
             dma((rows, n_chunks)),
         ],
@@ -335,16 +384,22 @@
     row1 = lax.broadcasted_iota(jnp.int32, (rows, 1), 0)
     stream1 = row1 // positions
     live = (g * GROUP + stream1) < live_ref[0]
-    dt = jax.nn.softplus(dtin + bias_ref[...])
-    decay = jnp.exp(-dt * rate_ref[...])
+
+    def padded(ref):
+        blank = jnp.zeros((1, dtin.shape[1] - ref.shape[1]), F32)
+        return jnp.concatenate([ref[...], blank], axis=1)
+
+    dt = jax.nn.softplus(dtin + padded(bias_ref))
+    decay = jnp.exp(-dt * padded(rate_ref))
+    sk_high, sk_low = split2(jnp.broadcast_to(padded(skip_ref), dt.shape))
     dt_high, dt_low = split2(dt)
     de_high, de_low = split2(decay)
     spread = jnp.dot(
-        jnp.concatenate([dt_high, dt_low, de_high, de_low], axis=0), spread_ref[...],
+        jnp.concatenate([dt_high, dt_low, de_high, de_low, sk_high, sk_low], axis=0), spread_ref[...],
         preferred_element_type=F32,
     )
     dt_wide = spread[:rows] + spread[rows : 2 * rows]
-    de_wide = spread[2 * rows : 3 * rows] + spread[3 * rows :]
+    de_wide = spread[2 * rows : 3 * rows] + spread[3 * rows : 4 * rows]
     u = jnp.where(live, dt_wide * x, 0.0)
     de_wide = jnp.where(live, de_wide, 1.0)
 
@@ -383,7 +438,7 @@
     dot_own = jnp.sum(bgate * cgate, -1, keepdims=True)
     dot_prev = jnp.sum(prev_b * cgate, -1, keepdims=True)
     y = keep * y + u * dot_own + jnp.where(second, de_wide * prev_u * dot_prev, 0.0)
-    y = y + skip_ref[...] * x
+    y = y + (spread[4 * rows : 5 * rows] + spread[5 * rows :]) * x
     gated = y * jax.nn.silu(zin)
     gated_ref[...] = (gated * gain_ref[...]).astype(BF16)
     sq_ref[...] = jnp.broadcast_to(jnp.sum(gated * gated, -1, keepdims=True), sq_ref.shape)
@@ -396,10 +451,7 @@
     heads_here = bias.shape[0]
     head_size = inner // heads_here
     spread = (jnp.arange(128)[:, None] == jnp.arange(inner)[None, :] // head_size).astype(BF16)
-    pad = ((0, 0), (0, 128 - heads_here))
-    bias = jnp.pad(bias.reshape(1, -1), pad)
-    rate = jnp.pad(rate.reshape(1, -1), pad)
-    skip = jnp.repeat(skip, head_size).reshape(1, -1)
+    bias, rate, skip = bias.reshape(1, -1), rate.reshape(1, -1), skip.reshape(1, -1)
 
     def up_spec(j):
         return pl.BlockSpec(

time: 99.1 us -> 96 us (0.969)
  Pallas kernels: 90.1 us -> 87.2 us
    unnamed x16 -> x22, local copies, waits for them, and re-layouts: 2.1 us -> 4.77 us
    pallas_call x1, Pallas kernels: 54.5 us -> 52.7 us  [project(): pl.pallas_call(functools.partial(project_kernel, heads, rows, float(width...]
    pad x2 -> x0, local copies, waits for them, and re-layouts: 1.32 us -> none  [the longest x1 0.66 us: scan(): bias = jnp.pad(bias.reshape(1, -1), pad)]
where the time goes in v2:
time: 96 us; the launch traced here: 95.4 us
  Pallas kernels  87.2 us (91%)
  local copies, waits for them, and re-layouts  6.7 us (7%)
  between operations  1.46 us (2%)
    pallas_call x1, Pallas kernels, project(): pl.pallas_call(functools.partial(project_kernel, heads, rows, float(width...  52.7 us
    pallas_call x1, Pallas kernels, output(): pl.pallas_call(functools.partial(output_kernel, heads, positions, float(i...  15.3 us
    pallas_call x1, Pallas kernels, scan(): pl.pallas_call(functools.partial(scan_kernel, positions), grid_spec=pltpu...  13.4 us
    pallas_call x1, Pallas kernels, front(): pl.pallas_call(functools.partial(front_kernel, capacity, positions), in_s...  5.75 us
    unnamed x22, local copies, waits for them, and re-layouts  4.77 us

profile of v2, /device:TPU:0, one launch (start us, length us, event | category | flops | bytes accessed | tf_op | source)
XLA Modules:
  0.0 95.4 jit_solution(7990663909274536792)
XLA Ops:
  0.6 0.0 copy-start.3
  1.3 0.1 fusion.spread_ref
  1.4 1.1 %reshape.62.hidden_ref = bf16[64,2048]{1,0:T(8,128)(2,1)S(1)} reshape(bf16[32,2,2048]{2,1,0:T(2,128)(2,1)} %param.16) | data formatting | bytes 524288 | tf_op jit(solution)/shard_map/reshape | solution.py:591
  2.4 0.0 copy-start.1
  2.5 3.4 %copy-done.1 = bf16[128,2048,16]{1,2,0:T(8,128)(2,1)S(1)} copy-done((bf16[128,2048,16]{1,2,0:T(8,128)(2,1)S(1)}, bf16[128,2048,16]{1,2,0:T(8,128)(2,1)}, u32[]{:S(2)}) %copy-start.1) | copy-done | bytes 8388632
  5.8 0.0 copy-start.4
  5.8 0.7 copy-done.4
  6.5 0.7 copy-done.6
  7.2 0.0 copy-start.8
  7.2 0.0 copy-start.9
  7.2 0.0 copy-start.10
  7.2 5.8 %front.1 = (bf16[64,2048]{1,0:T(8,128)(2,1)S(1)}, f32[64,128]{1,0:T(8,128)S(1)}) custom-call(s32[32]{0:T(128)S(1)} %copy-done.6, bf16[64,2048]{1,0:T(8,128)(2,1)S(1)} %reshape.62.hidden_ref, f32[1,2048]{1,0:T(1,128)S(1)} %bitcast.9, bf16[128,16,2048]{2,1,0:T(8,128)(2,1)S(1)} %bitcast.7), custom_call_target="tpu_custom_call" | custom-call | tf_op jit(solution)/shard_map/front/pallas_call | solution.py:66
  13.0 0.0 copy-done.3
  13.0 0.0 copy-done.2
  13.0 52.7 %project.1 = (f32[64,2432]{1,0:T(8,128)S(1)}, f32[64,128]{1,0:T(8,128)S(1)}) custom-call(bf16[64,2048]{1,0:T(8,128)(2,1)S(1)} %get-tuple-element.9.scaled_ref, f32[64,128]{1,0:T(8,128)S(1)} %get-tuple-element.10.stats_ref, bf16[2048,1024]{1,0:T(8,128)(2,1)} %wsig_ref.1, bf16[2048,1024]{1,0:T(8,128)(2,1)} %wgate_ref.1, bf16[16,2048]{1,0:T(8,128)(2,1)S(1)} %bitcast.8, ...), custom_call_target="tpu_custom_call" | custom-call | tf_op jit(solution)/shard_map/project/pallas_call | solution.py:327
  65.8 0.0 copy-done
  65.8 0.0 copy-done.5
  65.8 0.0 copy-done.7
  65.8 0.0 copy-done.8
  65.8 0.0 copy-done.9
  65.8 0.0 copy-done.10
  65.8 13.4 %scan.1 = (bf16[32,16,64,128]{3,2,1,0:T(8,128)(2,1)}, bf16[64,1024]{1,0:T(8,128)(2,1)S(1)}, f32[64,128]{1,0:T(8,128)S(1)}) custom-call(s32[32]{0:T(128)S(1)} %copy-done.7, s32[1]{0:T(128)S(6)} %copy.18.live_ref, f32[64,2432]{1,0:T(8,128)S(1)} %get-tuple-element.11.proj_ref, f32[64,128]{1,0:T(8,128)S(1)} %get-tuple-element.12.low_ref, f32[1,16]{1,0:T(1,128)S(1)} %bitcast.11, ...), custom_call_target="tpu_custom_call" | custom-call | tf_op jit(solution)/shard_map/scan/pallas_call | solution.py:469
  79.2 15.3 %output.1 = bf16[64,2048]{1,0:T(8,128)(2,1)S(1)} custom-call(s32[1]{0:T(128)S(6)} %copy.18.live_ref, bf16[64,1024]{1,0:T(8,128)(2,1)S(1)} %get-tuple-element.13.gated_ref, f32[64,128]{1,0:T(8,128)S(1)} %get-tuple-element.14.sq_ref, bf16[64,2048]{1,0:T(8,128)(2,1)S(1)} %reshape.62.hidden_ref, bf16[1024,8192]{1,0:T(8,128)(2,1)} %w_ref.1), custom_call_target="tpu_custom_call" | custom-call | tf_op jit(solution)/shard_map/output/pallas_call | solution.py:560
  94.5 0.9 reshape.68
  (6 shorter events, 0.0 us)
Async XLA Ops:
  0.6 12.4 %copy-start.3 = (bf16[2048,16]{0,1:T(8,128)(2,1)S(1)}, bf16[2048,16]{0,1:T(8,128)(2,1)}, u32[]{:S(2)}) copy-start(bf16[2048,16]{0,1:T(8,128)(2,1)} %param.20) | copy-start | bytes 196612
  2.4 3.4 %copy-start.1 = (bf16[128,2048,16]{1,2,0:T(8,128)(2,1)S(1)}, bf16[128,2048,16]{1,2,0:T(8,128)(2,1)}, u32[]{:S(2)}) copy-start(bf16[128,2048,16]{1,2,0:T(8,128)(2,1)} %param.26) | copy-start | bytes 25165828
  5.8 0.7 copy-start.4
  6.5 0.7 copy-start.6
  7.2 5.8 %copy-start.2 = (bf16[2048,256]{1,0:T(8,128)(2,1)S(1)}, bf16[2048,256]{1,0:T(8,128)(2,1)}, u32[]{:S(2)}) copy-start(bf16[2048,256]{1,0:T(8,128)(2,1)} %wbc_ref.1) | copy-start | bytes 3145732
  7.2 58.6 %copy-start = (bf16[128,16,1024]{2,1,0:T(8,128)(2,1)S(1)}, bf16[128,16,1024]{2,1,0:T(8,128)(2,1)}, u32[]{:S(2)}) copy-start(bf16[128,16,1024]{2,1,0:T(8,128)(2,1)} %rest_3_.1) | copy-start | bytes 12582916
  7.2 58.6 %copy-start.5 = (f32[1024]{0:T(1024)S(1)}, f32[1024]{0:T(1024)}, u32[]{:S(2)}) copy-start(f32[1024]{0:T(1024)} %param.25) | copy-start | bytes 12292
  7.2 58.6 %copy-start.7 = (s32[32]{0:T(128)S(1)}, s32[32]{0:T(128)}, u32[]{:S(2)}) copy-start(s32[32]{0:T(128)} %index_ref.3) | copy-start | bytes 388
  7.2 58.6 %copy-start.8 = (f32[16]{0:T(128)S(1)}, f32[16]{0:T(128)}, u32[]{:S(2)}) copy-start(f32[16]{0:T(128)} %param.22) | copy-start | bytes 196
  7.2 58.6 %copy-start.9 = (f32[16]{0:T(128)S(1)}, f32[16]{0:T(128)}, u32[]{:S(2)}) copy-start(f32[16]{0:T(128)} %param.23) | copy-start | bytes 196
  7.2 58.6 %copy-start.10 = (f32[16]{0:T(128)S(1)}, f32[16]{0:T(128)}, u32[]{:S(2)}) copy-start(f32[16]{0:T(128)} %param.24) | copy-start | bytes 196

commit v3 on v2

--- a/solution.py
+++ b/solution.py
@@ -75,7 +75,7 @@
             pltpu.VMEM((streams * rank, width), BF16),
             pltpu.SemaphoreType.DMA((streams,)),
         ],
-        compiler_params=pltpu.CompilerParams(vmem_limit_bytes=24 * 1024 * 1024),
+        compiler_params=pltpu.CompilerParams(vmem_limit_bytes=57 * 1024 * 1024),
         name="front",
     )(index, hidden, scale.reshape(1, -1), down)
 
@@ -84,7 +84,7 @@
     heads, rows, model_width, scaled_ref, stats_ref, wsig_ref, wgate_ref, wstep_ref, wbc_ref,
     proj_ref, low_ref,
     wsig, wgate, wstep, wbc, xbuf, pbuf, rup, rdown, sbuf,
-    w_sem, send_a, recv_a, send_b, recv_b, send_s, recv_s, send_r, recv_u, recv_d,
+    w_sem, send_a, recv_a, send_b, recv_b, send_f, recv_f, send_s, recv_s, send_r, recv_u, recv_d,
 ):
     h = lax.axis_index("head")
     r = lax.axis_index("row")
@@ -181,11 +181,30 @@
         row0 = lax.rem(r + e, rows) * tokens + k * prow
         return xbuf.at[pl.ds(pl.multiple_of(row0, 16), prow), :]
 
-    def b_copy(d, e, k):
+    chips = heads // 2
+    chip, core = h // 2, lax.rem(h, 2)
+    partner = chip * 2 + 1 - core
+
+    def owns(head):
+        return True if every == 1 else lax.rem(head, every) == 0
+
+    def b_copy(dx, e, k):
+        to = lax.rem(chip + dx, chips) * 2 + core if dx else partner
         return pltpu.make_async_remote_copy(
             src_ref=block_rows(e, k), dst_ref=block_rows(e, k),
-            send_sem=send_b.at[d, e], recv_sem=recv_b.at[d, e],
-            device_id={"head": lax.rem(h + d, heads)}, device_id_type=MESH,
+            send_sem=send_b.at[dx, e], recv_sem=recv_b.at[dx, e],
+            device_id={"head": to}, device_id_type=MESH,
+        )
+
+    def origin(dx, its_core):
+        return lax.rem(chip - dx + chips, chips) * 2 + its_core
+
+    def f_copy(dx, e, its_core):
+        block = block_rows(e, origin(dx, its_core) // every)
+        return pltpu.make_async_remote_copy(
+            src_ref=block, dst_ref=block,
+            send_sem=send_f.at[dx, e], recv_sem=recv_f.at[dx, e],
+            device_id={"head": partner}, device_id_type=MESH,
         )
 
     @when(is_owner)
@@ -198,16 +217,25 @@
                     pl.ds(j * width, width),
                 ]
                 pltpu.make_async_copy(dst, dst, recv_a.at[src_r * share + j]).wait()
-            for d in range(1, heads):
-                b_copy(d, e, piece).start()
+            for dx in list(range(1, chips)) + [0]:
+                b_copy(dx, e, piece).start()
 
     for e in range(rows):
-        for d in range(1, heads):
-            from_h = lax.rem(h - d + heads, heads)
-
-            @when(True if every == 1 else lax.rem(from_h, every) == 0)
+        for dx in range(1, chips):
+            @when(owns(origin(dx, core)))
             def _():
-                b_copy(d, e, from_h // every).wait_recv()
+                b_copy(dx, e, origin(dx, core) // every).wait_recv()
+                f_copy(dx, e, core).start()
+
+    for e in range(rows):
+        @when(owns(partner))
+        def _():
+            b_copy(0, e, partner // every).wait_recv()
+
+        for dx in range(1, chips):
+            @when(owns(origin(dx, 1 - core)))
+            def _():
+                f_copy(dx, e, 1 - core).wait_recv()
 
     bc_width = wbc.shape[1]
     half = min(inner, 512)
@@ -312,8 +340,14 @@
     @when(is_owner)
     def _():
         for e in range(rows):
-            for d in range(1, heads):
-                b_copy(d, e, piece).wait_send()
+            for dx in range(chips):
+                b_copy(dx, e, piece).wait_send()
+
+    for e in range(rows):
+        for dx in range(1, chips):
+            @when(owns(origin(dx, core)))
+            def _():
+                f_copy(dx, e, core).wait_send()
 
 
 def project(scaled, stats, wsig, wgate, wstep, wbc, heads, rows):
@@ -345,8 +379,10 @@
             dma((4,)),
             dma((pieces,)),
             dma((rows * share,)),
-            dma((heads, rows)),
-            dma((heads, rows)),
+            dma((heads // 2, rows)),
+            dma((heads // 2, rows)),
+            dma((heads // 2, rows)),
+            dma((heads // 2, rows)),
             dma((heads,)),
             dma((heads,)),
             dma((rows, n_chunks)),
@@ -492,11 +528,17 @@
 ):
     h = lax.axis_index("head")
     tokens, width = hidden_ref.shape
-    order = [d for d in range(1, heads)] + [0]
-    order = sorted(order, key=lambda d: (d == 0, abs(d - heads // 2)))
+    chips = heads // 2
+    chip, core = h // 2, lax.rem(h, 2)
+    partner = chip * 2 + 1 - core
+    order = [2 * dx + k for dx in list(range(1, chips)) + [0] for k in range(2)]
+
+    def target(d):
+        its_core = core if d % 2 else 1 - core
+        return lax.rem(chip + d // 2, chips) * 2 + its_core
 
     def load(d):
-        to = lax.rem(h + d, heads)
+        to = target(d)
         return pltpu.make_async_copy(
             w_ref.at[:, pl.ds(pl.multiple_of(to * width, 128), width)], wbuf.at[d], w_sem.at[d]
         )
@@ -525,21 +567,25 @@
             pbuf[d, :, c : c + step] = jnp.dot(
                 gated_ref[...], wbuf[d, :, c : c + step], preferred_element_type=F32
             ).astype(BF16)
-        if d:
-            copy = pltpu.make_async_remote_copy(
-                src_ref=pbuf.at[d], dst_ref=rbuf.at[d], send_sem=send_r.at[d],
-                recv_sem=recv_r.at[d],
-                device_id={"head": lax.rem(h + d, heads)}, device_id_type=MESH,
-            )
-            copy.start()
-            parts[d] = copy
+        if d == 1:
+            continue
+        if d % 2:
+            parts[d - 1].wait_recv()
+            pbuf[d] = (pbuf[d].astype(F32) + rbuf[d - 1].astype(F32)).astype(BF16)
+        copy = pltpu.make_async_remote_copy(
+            src_ref=pbuf.at[d], dst_ref=rbuf.at[d], send_sem=send_r.at[d],
+            recv_sem=recv_r.at[d],
+            device_id={"head": target(d) if d % 2 else partner}, device_id_type=MESH,
+        )
+        copy.start()
+        parts[d] = copy
     square = sq_ref[...]
     for d in range(1, heads):
         copies[d - 1].wait_recv()
         square = square + sbuf[d]
     inverse = lax.rsqrt(square[:, :1] / inner_width + EPSILON)
-    mixer = pbuf[0].astype(F32)
-    for d in sorted(parts, key=lambda d: -abs(d - heads // 2)):
+    mixer = pbuf[1].astype(F32)
+    for d in [0] + [2 * dx + 1 for dx in range(1, chips)]:
         parts[d].wait_recv()
         mixer = mixer + rbuf[d].astype(F32)
     stream = lax.broadcasted_iota(jnp.int32, (tokens, 1), 0) // positions

time: 96 us -> 88 us (0.917)
  Pallas kernels: 87.2 us -> 81.5 us
  local copies, waits for them, and re-layouts: 6.7 us -> 4.38 us
    pallas_call x1, Pallas kernels: 15.3 us -> 11.3 us  [output(): pl.pallas_call(functools.partial(output_kernel, heads, positions, float(i...]
    unnamed x22, local copies, waits for them, and re-layouts: 4.77 us -> 1.74 us
    pallas_call x1, Pallas kernels: 52.7 us -> 51.7 us  [project(): pl.pallas_call(functools.partial(project_kernel, heads, rows, float(width...]
where the time goes in v3:
time: 88 us; the launch traced here: 87.5 us
  Pallas kernels  81.5 us (93%)
  local copies, waits for them, and re-layouts  4.38 us (5%)
  between operations  1.52 us (2%)
    pallas_call x1, Pallas kernels, project(): pl.pallas_call(functools.partial(project_kernel, heads, rows, float(width...  51.7 us
    pallas_call x1, Pallas kernels, scan(): pl.pallas_call(functools.partial(scan_kernel, positions), grid_spec=pltpu...  13.4 us
    pallas_call x1, Pallas kernels, output(): pl.pallas_call(functools.partial(output_kernel, heads, positions, float(i...  11.3 us
    pallas_call x1, Pallas kernels, front(): pl.pallas_call(functools.partial(front_kernel, capacity, positions), in_s...  5.2 us

profile of v3, /device:TPU:0, one launch (start us, length us, event | category | flops | bytes accessed | tf_op | source)
XLA Modules:
  0.0 87.5 jit_solution(4940962463294904750)
XLA Ops:
  0.6 0.0 copy-start.2
  0.6 0.0 copy-start.4
  1.4 0.1 fusion.spread_ref
  1.5 1.8 %reshape.62.hidden_ref = bf16[64,2048]{1,0:T(8,128)(2,1)} reshape(bf16[32,2,2048]{2,1,0:T(2,128)(2,1)} %param.16) | data formatting | bytes 524288 | tf_op jit(solution)/shard_map/reshape | solution.py:637
  3.2 0.0 copy-start.9
  3.2 0.0 copy-start.10
  3.2 5.2 %front.1 = (bf16[64,2048]{1,0:T(8,128)(2,1)}, f32[64,128]{1,0:T(8,128)}) custom-call(s32[32]{0:T(128)} %index_ref.3, bf16[64,2048]{1,0:T(8,128)(2,1)} %reshape.62.hidden_ref, f32[1,2048]{1,0:T(1,128)} %bitcast.13, bf16[128,16,2048]{2,1,0:T(8,128)(2,1)} %bitcast.12), custom_call_target="tpu_custom_call" | custom-call | tf_op jit(solution)/shard_map/front/pallas_call | solution.py:66
  8.5 0.0 copy-done.2
  8.5 0.0 copy-done.4
  8.5 0.0 copy-start.3
  8.5 0.9 %copy-done.3 = bf16[64,2048]{1,0:T(8,128)(2,1)S(1)} copy-done((bf16[64,2048]{1,0:T(8,128)(2,1)S(1)}, bf16[64,2048]{1,0:T(8,128)(2,1)}, u32[]{:S(2)}) %copy-start.3) | copy-done | bytes 262168
  9.4 0.8 copy-done.5
  10.2 51.7 %project.1 = (f32[64,2432]{1,0:T(8,128)S(1)}, f32[64,128]{1,0:T(8,128)S(1)}) custom-call(bf16[64,2048]{1,0:T(8,128)(2,1)S(1)} %copy-done.3, f32[64,128]{1,0:T(8,128)S(1)} %copy-done.5, bf16[2048,1024]{1,0:T(8,128)(2,1)} %wsig_ref.1, bf16[2048,1024]{1,0:T(8,128)(2,1)} %wgate_ref.1, bf16[16,2048]{1,0:T(8,128)(2,1)S(1)} %bitcast.7, bf16[2048,256]{1,0:T(8,128)(2,1)S(1)} %copy-done.2), custom_call_target="tpu_custom_call" | custom-call | tf_op jit(solution)/shard_map/project/pallas_call | solution.py:361
  61.9 0.0 copy-done
  61.9 0.0 copy-done.6
  61.9 0.0 copy-done.7
  61.9 0.0 copy-done.8
  61.9 0.0 copy-done.9
  61.9 0.0 copy-done.10
  61.9 0.0 copy-start.1
  61.9 13.4 %scan.1 = (bf16[32,16,64,128]{3,2,1,0:T(8,128)(2,1)}, bf16[64,1024]{1,0:T(8,128)(2,1)S(1)}, f32[64,128]{1,0:T(8,128)S(1)}) custom-call(s32[32]{0:T(128)S(1)} %copy-done.7, s32[1]{0:T(128)S(6)} %copy.18.live_ref, f32[64,2432]{1,0:T(8,128)S(1)} %get-tuple-element.11.proj_ref, f32[64,128]{1,0:T(8,128)S(1)} %get-tuple-element.12.low_ref, f32[1,16]{1,0:T(1,128)S(1)} %bitcast.9, ...), custom_call_target="tpu_custom_call" | custom-call | tf_op jit(solution)/shard_map/scan/pallas_call | solution.py:505
  75.3 0.0 copy-done.1
  75.3 11.3 %output.1 = bf16[64,2048]{1,0:T(8,128)(2,1)S(1)} custom-call(s32[1]{0:T(128)S(6)} %copy.18.live_ref, bf16[64,1024]{1,0:T(8,128)(2,1)S(1)} %get-tuple-element.13.gated_ref, f32[64,128]{1,0:T(8,128)S(1)} %get-tuple-element.14.sq_ref, bf16[64,2048]{1,0:T(8,128)(2,1)S(1)} %copy-done.1, bf16[1024,8192]{1,0:T(8,128)(2,1)} %w_ref.1), custom_call_target="tpu_custom_call" | custom-call | tf_op jit(solution)/shard_map/output/pallas_call | solution.py:606
  86.6 0.9 %reshape.68 = bf16[32,2,2048]{2,1,0:T(2,128)(2,1)} reshape(bf16[64,2048]{1,0:T(8,128)(2,1)S(1)} %output.1) | data formatting | bytes 524288 | tf_op jit(solution)/shard_map/reshape | solution.py:649
  (6 shorter events, 0.0 us)
Async XLA Ops:
  0.6 7.8 %copy-start.2 = (bf16[2048,256]{1,0:T(8,128)(2,1)S(1)}, bf16[2048,256]{1,0:T(8,128)(2,1)}, u32[]{:S(2)}) copy-start(bf16[2048,256]{1,0:T(8,128)(2,1)} %wbc_ref.1) | copy-start | bytes 3145732
  0.6 7.8 %copy-start.4 = (bf16[2048,16]{0,1:T(8,128)(2,1)S(1)}, bf16[2048,16]{0,1:T(8,128)(2,1)}, u32[]{:S(2)}) copy-start(bf16[2048,16]{0,1:T(8,128)(2,1)} %param.20) | copy-start | bytes 196612
  3.2 58.7 %copy-start = (bf16[128,16,1024]{2,1,0:T(8,128)(2,1)S(1)}, bf16[128,16,1024]{2,1,0:T(8,128)(2,1)}, u32[]{:S(2)}) copy-start(bf16[128,16,1024]{2,1,0:T(8,128)(2,1)} %rest_3_.1) | copy-start | bytes 12582916
  3.2 58.7 %copy-start.6 = (f32[1024]{0:T(1024)S(1)}, f32[1024]{0:T(1024)}, u32[]{:S(2)}) copy-start(f32[1024]{0:T(1024)} %param.25) | copy-start | bytes 12292
  3.2 58.7 %copy-start.7 = (s32[32]{0:T(128)S(1)}, s32[32]{0:T(128)}, u32[]{:S(2)}) copy-start(s32[32]{0:T(128)} %index_ref.3) | copy-start | bytes 388
  3.2 58.7 %copy-start.8 = (f32[16]{0:T(128)S(1)}, f32[16]{0:T(128)}, u32[]{:S(2)}) copy-start(f32[16]{0:T(128)} %param.22) | copy-start | bytes 196
  3.2 58.7 %copy-start.9 = (f32[16]{0:T(128)S(1)}, f32[16]{0:T(128)}, u32[]{:S(2)}) copy-start(f32[16]{0:T(128)} %param.23) | copy-start | bytes 196
  3.2 58.7 %copy-start.10 = (f32[16]{0:T(128)S(1)}, f32[16]{0:T(128)}, u32[]{:S(2)}) copy-start(f32[16]{0:T(128)} %param.24) | copy-start | bytes 196
  8.5 1.0 %copy-start.3 = (bf16[64,2048]{1,0:T(8,128)(2,1)S(1)}, bf16[64,2048]{1,0:T(8,128)(2,1)}, u32[]{:S(2)}) copy-start(bf16[64,2048]{1,0:T(8,128)(2,1)} %get-tuple-element.9.scaled_ref) | copy-start | bytes 786436
  9.4 0.8 copy-start.5
  61.9 13.4 %copy-start.1 = (bf16[64,2048]{1,0:T(8,128)(2,1)S(1)}, bf16[64,2048]{1,0:T(8,128)(2,1)}, u32[]{:S(2)}) copy-start(bf16[64,2048]{1,0:T(8,128)(2,1)} %reshape.62.hidden_ref) | copy-start | bytes 786436

commit v4 on v3

--- a/solution.py
+++ b/solution.py
@@ -238,7 +238,7 @@
                 f_copy(dx, e, 1 - core).wait_recv()
 
     bc_width = wbc.shape[1]
-    half = min(inner, 512)
+    half = min(inner, 256)
     chunks = [(wbc, 0, bc_width, 2 * inner, 0), (wstep, None, 128, 2 * inner + bc_width, 1)]
     for i, w in ((2, wsig), (3, wgate)):
         for c in range(0, inner, half):
@@ -356,7 +356,7 @@
     out_width = 2 * inner + wbc.shape[1] + 128
     share = heads // rows
     pieces = min(heads, tokens // 16)
-    n_chunks = 2 + 2 * (inner // min(inner, 512))
+    n_chunks = 2 + 2 * (inner // min(inner, 256))
     dma = pltpu.SemaphoreType.DMA
     return pl.pallas_call(
         functools.partial(project_kernel, heads, rows, float(width * heads)),

time: 88 us -> 88.6 us (level)
  no operation moved by 1% of the time
where the time goes in v4:
time: 88.6 us; the launch traced here: 88.1 us
  Pallas kernels  82.2 us (93%)
  local copies, waits for them, and re-layouts  4.38 us (5%)
  between operations  1.52 us (2%)
    pallas_call x1, Pallas kernels, project(): pl.pallas_call(functools.partial(project_kernel, heads, rows, float(width...  52.4 us
    pallas_call x1, Pallas kernels, scan(): pl.pallas_call(functools.partial(scan_kernel, positions), grid_spec=pltpu...  13.4 us
    pallas_call x1, Pallas kernels, output(): pl.pallas_call(functools.partial(output_kernel, heads, positions, float(i...  11.3 us
    pallas_call x1, Pallas kernels, front(): pl.pallas_call(functools.partial(front_kernel, capacity, positions), in_s...  5.2 us

profile of v4, /device:TPU:0, one launch (start us, length us, event | category | flops | bytes accessed | tf_op | source)
XLA Modules:
  0.0 88.1 jit_solution(13932619843952549594)
XLA Ops:
  0.6 0.0 copy-start.2
  0.6 0.0 copy-start.4
  1.4 0.1 fusion.spread_ref
  1.5 1.8 %reshape.62.hidden_ref = bf16[64,2048]{1,0:T(8,128)(2,1)} reshape(bf16[32,2,2048]{2,1,0:T(2,128)(2,1)} %param.16) | data formatting | bytes 524288 | tf_op jit(solution)/shard_map/reshape | solution.py:637
  3.2 0.0 copy-start.9
  3.2 0.0 copy-start.10
  3.2 5.2 %front.1 = (bf16[64,2048]{1,0:T(8,128)(2,1)}, f32[64,128]{1,0:T(8,128)}) custom-call(s32[32]{0:T(128)} %index_ref.3, bf16[64,2048]{1,0:T(8,128)(2,1)} %reshape.62.hidden_ref, f32[1,2048]{1,0:T(1,128)} %bitcast.13, bf16[128,16,2048]{2,1,0:T(8,128)(2,1)} %bitcast.12), custom_call_target="tpu_custom_call" | custom-call | tf_op jit(solution)/shard_map/front/pallas_call | solution.py:66
  8.5 0.0 copy-done.2
  8.5 0.0 copy-done.4
  8.5 0.0 copy-start.3
  8.5 0.9 %copy-done.3 = bf16[64,2048]{1,0:T(8,128)(2,1)S(1)} copy-done((bf16[64,2048]{1,0:T(8,128)(2,1)S(1)}, bf16[64,2048]{1,0:T(8,128)(2,1)}, u32[]{:S(2)}) %copy-start.3) | copy-done | bytes 262168
  9.4 0.8 copy-done.5
  10.2 52.4 %project.1 = (f32[64,2432]{1,0:T(8,128)S(1)}, f32[64,128]{1,0:T(8,128)S(1)}) custom-call(bf16[64,2048]{1,0:T(8,128)(2,1)S(1)} %copy-done.3, f32[64,128]{1,0:T(8,128)S(1)} %copy-done.5, bf16[2048,1024]{1,0:T(8,128)(2,1)} %wsig_ref.1, bf16[2048,1024]{1,0:T(8,128)(2,1)} %wgate_ref.1, bf16[16,2048]{1,0:T(8,128)(2,1)S(1)} %bitcast.7, bf16[2048,256]{1,0:T(8,128)(2,1)S(1)} %copy-done.2), custom_call_target="tpu_custom_call" | custom-call | tf_op jit(solution)/shard_map/project/pallas_call | solution.py:361
  62.5 0.0 copy-done
  62.6 0.0 copy-done.6
  62.6 0.0 copy-done.7
  62.6 0.0 copy-done.8
  62.6 0.0 copy-done.9
  62.6 0.0 copy-done.10
  62.6 0.0 copy-start.1
  62.6 13.4 %scan.1 = (bf16[32,16,64,128]{3,2,1,0:T(8,128)(2,1)}, bf16[64,1024]{1,0:T(8,128)(2,1)S(1)}, f32[64,128]{1,0:T(8,128)S(1)}) custom-call(s32[32]{0:T(128)S(1)} %copy-done.7, s32[1]{0:T(128)S(6)} %copy.18.live_ref, f32[64,2432]{1,0:T(8,128)S(1)} %get-tuple-element.11.proj_ref, f32[64,128]{1,0:T(8,128)S(1)} %get-tuple-element.12.low_ref, f32[1,16]{1,0:T(1,128)S(1)} %bitcast.9, ...), custom_call_target="tpu_custom_call" | custom-call | tf_op jit(solution)/shard_map/scan/pallas_call | solution.py:505
  76.0 0.0 copy-done.1
  76.0 11.3 %output.1 = bf16[64,2048]{1,0:T(8,128)(2,1)S(1)} custom-call(s32[1]{0:T(128)S(6)} %copy.18.live_ref, bf16[64,1024]{1,0:T(8,128)(2,1)S(1)} %get-tuple-element.13.gated_ref, f32[64,128]{1,0:T(8,128)S(1)} %get-tuple-element.14.sq_ref, bf16[64,2048]{1,0:T(8,128)(2,1)S(1)} %copy-done.1, bf16[1024,8192]{1,0:T(8,128)(2,1)} %w_ref.1), custom_call_target="tpu_custom_call" | custom-call | tf_op jit(solution)/shard_map/output/pallas_call | solution.py:606
  87.3 0.9 %reshape.68 = bf16[32,2,2048]{2,1,0:T(2,128)(2,1)} reshape(bf16[64,2048]{1,0:T(8,128)(2,1)S(1)} %output.1) | data formatting | bytes 524288 | tf_op jit(solution)/shard_map/reshape | solution.py:649
  (6 shorter events, 0.0 us)
Async XLA Ops:
  0.6 7.8 %copy-start.2 = (bf16[2048,256]{1,0:T(8,128)(2,1)S(1)}, bf16[2048,256]{1,0:T(8,128)(2,1)}, u32[]{:S(2)}) copy-start(bf16[2048,256]{1,0:T(8,128)(2,1)} %wbc_ref.1) | copy-start | bytes 3145732
  0.6 7.8 %copy-start.4 = (bf16[2048,16]{0,1:T(8,128)(2,1)S(1)}, bf16[2048,16]{0,1:T(8,128)(2,1)}, u32[]{:S(2)}) copy-start(bf16[2048,16]{0,1:T(8,128)(2,1)} %param.20) | copy-start | bytes 196612
  3.2 59.3 %copy-start = (bf16[128,16,1024]{2,1,0:T(8,128)(2,1)S(1)}, bf16[128,16,1024]{2,1,0:T(8,128)(2,1)}, u32[]{:S(2)}) copy-start(bf16[128,16,1024]{2,1,0:T(8,128)(2,1)} %rest_3_.1) | copy-start | bytes 12582916
  3.2 59.3 %copy-start.6 = (f32[1024]{0:T(1024)S(1)}, f32[1024]{0:T(1024)}, u32[]{:S(2)}) copy-start(f32[1024]{0:T(1024)} %param.25) | copy-start | bytes 12292
  3.2 59.4 %copy-start.7 = (s32[32]{0:T(128)S(1)}, s32[32]{0:T(128)}, u32[]{:S(2)}) copy-start(s32[32]{0:T(128)} %index_ref.3) | copy-start | bytes 388
  3.2 59.4 %copy-start.8 = (f32[16]{0:T(128)S(1)}, f32[16]{0:T(128)}, u32[]{:S(2)}) copy-start(f32[16]{0:T(128)} %param.22) | copy-start | bytes 196
  3.2 59.4 %copy-start.9 = (f32[16]{0:T(128)S(1)}, f32[16]{0:T(128)}, u32[]{:S(2)}) copy-start(f32[16]{0:T(128)} %param.23) | copy-start | bytes 196
  3.2 59.4 %copy-start.10 = (f32[16]{0:T(128)S(1)}, f32[16]{0:T(128)}, u32[]{:S(2)}) copy-start(f32[16]{0:T(128)} %param.24) | copy-start | bytes 196
  8.5 1.0 %copy-start.3 = (bf16[64,2048]{1,0:T(8,128)(2,1)S(1)}, bf16[64,2048]{1,0:T(8,128)(2,1)}, u32[]{:S(2)}) copy-start(bf16[64,2048]{1,0:T(8,128)(2,1)} %get-tuple-element.9.scaled_ref) | copy-start | bytes 786436
  9.4 0.8 copy-start.5
  62.6 13.4 %copy-start.1 = (bf16[64,2048]{1,0:T(8,128)(2,1)S(1)}, bf16[64,2048]{1,0:T(8,128)(2,1)}, u32[]{:S(2)}) copy-start(bf16[64,2048]{1,0:T(8,128)(2,1)} %reshape.62.hidden_ref) | copy-start | bytes 786436
